TPU v7x, 1024 devices: a whole 4x4x32 slice. The times are simulated.
1024 devices in a mesh: row: 32 (over z), col: 32 (over x, y, core).
Axes of the slice: x: 4, y: 4, z: 32, core: 2. Of those that a mesh axis runs over, the one named last changes fastest.
Arguments:
- momentum: float32 [16384, 16384], P('row', 'col'), may hold values from -18 to 18
- gradient: bfloat16 [16384, 16384], P('row', 'col'), may hold values from -6 to 6
- right_factor: float32 [16384, 64], P('col'), may hold values from -1 to 1
Outputs:
- update: bfloat16 [16384, 16384], P('row', 'col')
- left: float32 [16384, 64], P('row')
- normed: float32 [16384, 64], P('col')
- new_momentum: float32 [16384, 16384], P('row', 'col')
- first_factor: float32 [64, 64], replicated
All inputs are finite; a program needn't handle non-finite values.
Results may differ from a plain program's by a relative error of at most 0.001.
Values sent between devices are 32-bit elements; how exact they have to be, the bound alone decides.
No kernel may reach another device: no remote copies, remote signals or barrier semaphores. Data moves between devices by JAX's collectives and lax.ppermute only.
A program may use at most 32 MiB of HBM per device.

v0:
```python
import jax
import jax.numpy as jnp
from jax import lax
from jax.sharding import PartitionSpec as P

NROW = 16384
NCOL = 16384
RANK = 64


HIGH = lax.Precision.HIGHEST


def gram_of(block):
    return jnp.dot(block.T, block, precision=HIGH, preferred_element_type=jnp.float32)


def apply_lower(block, lower):
    return lax.linalg.triangular_solve(lower, block, left_side=False, lower=True, transpose_a=True)


def right_part(blended, factor):
    return lax.dot_general(
        blended,
        factor,
        (((0,), (0,)), ((), ())),
        precision=HIGH,
        preferred_element_type=jnp.float32,
    )


def on_device(momentum, gradient, right_factor):
    blended = momentum + gradient.astype(jnp.float32)
    partial_value = jnp.dot(
        blended, right_factor, precision=HIGH, preferred_element_type=jnp.float32
    )
    left_raw = lax.psum(partial_value, "col")
    gram_one = lax.psum(gram_of(left_raw), "row")
    lower_one = jnp.linalg.cholesky(gram_one)
    left_one = apply_lower(left_raw, lower_one)
    first_factor = lower_one / jnp.sqrt(jnp.float32(NROW) * jnp.float32(NCOL))
    gram_two = lax.psum(gram_of(left_one), "row")
    lower_two = jnp.linalg.cholesky(gram_two)
    left = apply_lower(left_one, lower_two)
    right = lax.psum(right_part(blended, left), "row")
    squares = lax.psum(jnp.sum(right * right, axis=0), "col")
    normed = right / (jnp.sqrt(squares) + 1e-06)
    scale = jnp.sqrt(jnp.float32(NROW) * jnp.float32(NCOL) / jnp.float32(RANK))
    update = (
        scale * jnp.dot(left, normed.T, precision=HIGH, preferred_element_type=jnp.float32)
    ).astype(jnp.bfloat16)
    new_momentum = blended - 0.05 * jnp.dot(
        left, right.T, precision=HIGH, preferred_element_type=jnp.float32
    )
    return (update, left, normed, new_momentum, first_factor)


def solution(mesh):
    in_specs = (P("row", "col"), P("row", "col"), P("col", None))
    out_specs = (P("row", "col"), P("row", None), P("col", None), P("row", "col"), P())
    return jax.shard_map(
        on_device, mesh=mesh, in_specs=in_specs, out_specs=out_specs, check_vma=False
    )
```

profile of v0, /device:TPU:1, one launch (start us, length us, event | category | flops | bytes accessed | tf_op | source)
XLA Modules:
  0.0 769.8 jit_solution(464441190065399527)
XLA Ops:
  7.2 0.0 copy-start
  7.2 0.0 all-reduce.3.cloned.1.call-start
  7.2 0.8 copy-done
  8.1 3.2 fusion.3
  11.3 0.0 copy-start.1
  11.3 0.0 all-reduce.3.cloned.1.call-update
  11.3 0.0 all-reduce.5.cloned.1.call-start
  11.4 181.9 %all-reduce.3.cloned.1.call-done = f32[512,64]{0,1:T(8,128)} async-done(((f32[512,64]{0,1:T(8,128)}), f32[512,64]{0,1:T(8,128)}) %all-reduce.3.cloned.1.call-update) | async-done | bytes 131088 | tf_op jit(solution)/shard_map/psum | solution.py:37
  193.3 1.2 fusion.15
  194.5 83.7 %psum.36 = f32[64,64]{0,1:T(8,128)S(1)} all-reduce(f32[64,64]{0,1:T(8,128)S(1)} %fusion.15), channel_id=1, replica_groups=mesh['row'=32,'col'=32] {'row'}, use_global_device_ids=true, to_apply=%region_1.0 | all-reduce | flops 4096 | bytes 32768 | tf_op jit(solution)/shard_map/psum | solution.py:38
  278.2 0.1 copy.9
  278.3 5.8 cholesky.44
  284.2 0.6 compare_reduce_fusion.1
  284.8 1.3 fusion.14
  286.1 4.9 custom-call.6
  291.0 1.2 convolution_bitcast_fusion.1
  292.2 0.0 copy-start.2
  292.2 0.3 fusion.16
  292.5 77.9 %psum.37 = f32[64,64]{0,1:T(8,128)S(1)} all-reduce(f32[64,64]{0,1:T(8,128)S(1)} %fusion.16), channel_id=1, replica_groups=mesh['row'=32,'col'=32] {'row'}, use_global_device_ids=true, to_apply=%region_4.7 | all-reduce | flops 4096 | bytes 32768 | tf_op jit(solution)/shard_map/psum | solution.py:42
  370.4 0.1 copy.11
  370.5 5.8 cholesky.55
  376.4 0.6 compare_reduce_fusion
  377.1 0.7 fusion.4
  377.7 4.9 custom-call.7
  382.6 0.3 convolution_bitcast_fusion
  383.0 0.0 copy-done.1
  383.0 0.0 copy-done.2
  383.0 0.0 copy-start.3
  383.0 1.5 fusion.2
  384.5 0.0 all-reduce.5.cloned.1.call-update
  384.5 288.4 %all-reduce.5.cloned.1.call-done = f32[512,64]{0,1:T(8,128)} async-done(((f32[512,64]{0,1:T(8,128)}), f32[512,64]{0,1:T(8,128)}) %all-reduce.5.cloned.1.call-update) | async-done | bytes 131088 | tf_op jit(solution)/shard_map/psum | solution.py:45
  672.9 0.0 copy-start.4
  672.9 1.1 multiply_reduce_fusion
  674.0 84.9 %psum.39 = f32[64]{0:T(128)S(1)} all-reduce(f32[64]{0:T(128)S(1)} %multiply_reduce_fusion), channel_id=1, replica_groups=mesh['row'=32,'col'=32] {'col'}, use_global_device_ids=true, to_apply=%region_7.10 | all-reduce | flops 64 | bytes 512 | tf_op jit(solution)/shard_map/psum | solution.py:46
  758.9 0.0 copy-done.4
  758.9 0.1 broadcast_divide_fusion
  759.0 0.0 copy-start.5
  759.0 1.8 fusion.1
  760.8 0.0 copy-done.3
  760.8 0.0 copy-done.5
  760.9 2.1 fusion
  (5 shorter events, 0.1 us)
Async XLA Ops:
  7.2 0.9 copy-start
  7.2 186.1 %all-reduce.3.cloned.1.call-start = ((), (), s32[]{:S(2)}) async-start(), calls=%async_computation | async-start | bytes 262144 | tf_op jit(solution)/shard_map/psum | solution.py:37
  11.3 371.7 %copy-start.1 = (f32[512,512]{1,0:T(8,128)S(1)}, f32[512,512]{1,0:T(8,128)}, u32[]{:S(2)}) copy-start(f32[512,512]{1,0:T(8,128)} %param.6) | copy-start | bytes 3145732
  11.3 661.6 %all-reduce.5.cloned.1.call-start = ((), (), s32[]{:S(2)}) async-start(), calls=%async_computation.1 | async-start | bytes 262144 | tf_op jit(solution)/shard_map/psum | solution.py:45
  292.2 90.7 %copy-start.2 = (bf16[512,512]{1,0:T(8,128)(2,1)S(1)}, bf16[512,512]{1,0:T(8,128)(2,1)}, u32[]{:S(2)}) copy-start(bf16[512,512]{1,0:T(8,128)(2,1)} %param.7) | copy-start | bytes 1572868
  383.0 377.9 %copy-start.3 = (f32[512,64]{0,1:T(8,128)}, f32[512,64]{0,1:T(8,128)S(1)}, u32[]{:S(2)}) copy-start(f32[512,64]{0,1:T(8,128)S(1)} %convolution_bitcast_fusion) | copy-start | bytes 393220
  672.9 86.0 %copy-start.4 = (f32[512,64]{0,1:T(8,128)S(1)}, f32[512,64]{0,1:T(8,128)}, u32[]{:S(2)}) copy-start(f32[512,64]{0,1:T(8,128)} %all-reduce.5.cloned.1.call-done) | copy-start | bytes 393220
  759.0 1.9 copy-start.5
Sparse Core Ops, SparseCore 0:
  11.8 181.4 all-reduce.2
  384.6 288.2 all-reduce.4
where the time goes:
time: 770 us
  waiting for transfers between devices  470 us (61%)
  blocking collectives  247 us (32%)
  other arithmetic  26 us (3%)
  between operations  14.2 us (2%)
  matrix products  11.7 us (2%)
    psum x1, waiting for transfers between devices, on_device(): right = lax.psum(right_part(blended, left), 'row')  288 us
    psum x1, waiting for transfers between devices, on_device(): left_raw = lax.psum(partial_value, 'col')  182 us
    psum x1, blocking collectives, on_device(): squares = lax.psum(jnp.sum(right * right, axis=0), 'col')  84.9 us
    psum x1, blocking collectives, on_device(): gram_one = lax.psum(gram_of(left_raw), 'row')  83.7 us
    psum x1, blocking collectives, on_device(): gram_two = lax.psum(gram_of(left_one), 'row')  77.9 us
  transfers between devices with their start and end apart: 2, of which 2 were waited for; matrix products, arithmetic and copies ran while one was open for 0% of the time, Pallas kernels for 0%

commit v1 on v0

v1 whole, which is shorter than its diff:
```python
import jax
import jax.numpy as jnp
from jax import lax
from jax.sharding import Mesh, PartitionSpec as P

NROW = 16384
NCOL = 16384
RANK = 64
HIGH = lax.Precision.HIGHEST
COL = ("x", "y", "core")
NEAR = ("near",)
FAR = ("far",)


def dot(a, b, dims):
    return lax.dot_general(
        a, b, (dims, ((), ())), precision=HIGH, preferred_element_type=jnp.float32
    )


def nn(a, b):
    return dot(a, b, ((1,), (0,)))


def nt(a, b):
    return dot(a, b, ((1,), (1,)))


def to_tiles(a):
    return a.reshape(8, 8, 4, 128).transpose(0, 2, 1, 3).reshape(32, 8, 128)


def from_tiles(t):
    return t.reshape(8, 4, 8, 128).transpose(0, 2, 1, 3).reshape(64, 512)


def exchange(chunks, axes):
    return lax.all_to_all(chunks, axes, 0, 0, tiled=True)


def spread(chunk, n, axes):
    copies = jnp.broadcast_to(chunk[None], (n,) + chunk.shape)
    return exchange(lax.optimization_barrier(copies), axes)


def lower_and_inverse(gram):
    lower = jnp.linalg.cholesky(gram)
    inverse = lax.linalg.triangular_solve(
        lower, jnp.eye(RANK, dtype=jnp.float32), left_side=True, lower=True
    )
    return lower, inverse


def on_device(momentum, gradient, right_factor):
    blended = momentum + gradient.astype(jnp.float32)
    factor_t = right_factor.T
    part = to_tiles(nt(factor_t, blended))
    mine = jnp.sum(exchange(part, COL), axis=0)
    left_raw_t = from_tiles(spread(mine, 32, COL))
    product = to_tiles(nn(left_raw_t, blended)).reshape(256, 128)
    gram = nt(left_raw_t, left_raw_t)
    gram = jnp.concatenate([gram[:32], gram[32:]], axis=1)
    send = jnp.concatenate([product, gram], axis=0).reshape(4, 72, 128)
    near = jnp.sum(exchange(send, NEAR), axis=0)
    total = spread(lax.psum(near, FAR), 4, NEAR).reshape(288, 128)
    product_t = from_tiles(total[:256].reshape(32, 8, 128))
    gram_one = jnp.concatenate([total[256:, :64], total[256:, 64:]], axis=0)
    gram_one = (gram_one + gram_one.T) / 2
    lower_one, inverse_one = lower_and_inverse(gram_one)
    first_factor = lower_one / jnp.sqrt(jnp.float32(NROW) * jnp.float32(NCOL))
    factor_one = nn(inverse_one, factor_t)
    right_one = nn(inverse_one, product_t)
    pair = jnp.concatenate([nt(factor_one, right_one), nt(right_one, right_one)], axis=1)
    pair = jnp.sum(spread(pair, 32, COL), axis=0)
    gram_two, squared = pair[:, :64], pair[:, 64:]
    gram_two = (gram_two + gram_two.T) / 2
    _, inverse_two = lower_and_inverse(gram_two)
    left_one = nn(inverse_one, left_raw_t)
    left_t = nn(inverse_two, left_one)
    right_t = nn(inverse_two, right_one)
    squares = jnp.sum(nn(inverse_two, squared) * inverse_two, axis=1)
    normed_t = right_t / (jnp.sqrt(squares) + 1e-06)[:, None]
    scale = jnp.sqrt(jnp.float32(NROW) * jnp.float32(NCOL) / jnp.float32(RANK))
    tn = lambda a, b: dot(a, b, ((0,), (0,)))
    update = (scale * tn(left_t, normed_t)).astype(jnp.bfloat16)
    new_momentum = blended - 0.05 * tn(left_t, right_t)
    return (update, left_t.T, normed_t.T, new_momentum, first_factor)


def solution(mesh):
    names = FAR + NEAR + COL
    inner = Mesh(mesh.devices.reshape(8, 4, 4, 4, 2), names)
    row, col = FAR + NEAR, COL
    in_specs = (P(row, col), P(row, col), P(col, None))
    out_specs = (P(row, col), P(row, None), P(col, None), P(row, col), P())
    return jax.shard_map(
        on_device, mesh=inner, in_specs=in_specs, out_specs=out_specs, check_vma=False
    )
```

time: 770 us -> 166 us (0.22)
  waiting for transfers between devices: 470 us -> 21.8 us
  blocking collectives: 247 us -> 84 us
  starting transfers between devices: 0.08 us -> 16.8 us
  between operations: 14.2 us -> 0.88 us
    psum x2 -> x0, waiting for transfers between devices: 470 us -> none  [the longest x1 288 us: on_device(): right = lax.psum(right_part(blended, left), 'row')]
    psum x3 -> x1, blocking collectives: 247 us -> 42.3 us  [on_device(): total = spread(lax.psum(near, FAR), 4, NEAR).reshape(288, 128)]
    all_to_all x0 -> x3, blocking collectives: none -> 41.7 us  [exchange(): return lax.all_to_all(chunks, axes, 0, 0, tiled=True)]
    all_to_all x0 -> x2, waiting for transfers between devices: none -> 21.8 us  [exchange(): return lax.all_to_all(chunks, axes, 0, 0, tiled=True)]
    all_to_all x0 -> x2, starting transfers between devices: none -> 16.8 us  [exchange(): return lax.all_to_all(chunks, axes, 0, 0, tiled=True)]
  transfers between devices with their start and end apart: 2 -> 2, of which waited for: 2 -> 2; matrix products, arithmetic and copies ran while one was open for 0% -> 2% of each run, Pallas kernels for 0% -> 0%
where the time goes in v1:
time: 166 us
  blocking collectives  84 us (51%)
  other arithmetic  27 us (16%)
  waiting for transfers between devices  21.8 us (13%)
  starting transfers between devices  16.8 us (10%)
  matrix products  10.6 us (6%)
  local copies, waits for them, and re-layouts  4.62 us (3%)
    psum x1, blocking collectives, on_device(): total = spread(lax.psum(near, FAR), 4, NEAR).reshape(288, 128)  42.3 us
    all_to_all x3, blocking collectives, exchange(): return lax.all_to_all(chunks, axes, 0, 0, tiled=True)  41.7 us
    all_to_all x2, waiting for transfers between devices, exchange(): return lax.all_to_all(chunks, axes, 0, 0, tiled=True)  21.8 us
    all_to_all x2, starting transfers between devices, exchange(): return lax.all_to_all(chunks, axes, 0, 0, tiled=True)  16.8 us
    another operation x6, other arithmetic, lower_and_inverse(): lower = jnp.linalg.cholesky(gram)  13 us
    another operation x3, other arithmetic, lower_and_inverse(): lax.linalg.triangular_solve(lower, jnp.eye(RANK, dtype=jnp.float32), left...  10.4 us
    dot_general x13, matrix products, dot(): lax.dot_general(a, b, (dims, ((), ())), precision=HIGH, preferred_element...  10.1 us
  transfers between devices with their start and end apart: 2, of which 2 were waited for; matrix products, arithmetic and copies ran while one was open for 2% of the time, Pallas kernels for 0%

profile of v1, /device:TPU:1, one launch (start us, length us, event | category | flops | bytes accessed | tf_op | source)
XLA Modules:
  0.0 165.7 jit_solution(12959903242237177624)
XLA Ops:
  0.6 0.0 copy-start
  0.6 0.0 copy-start.1
  0.7 0.9 copy-done
  1.5 2.5 %fusion.4 = f32[512,64]{0,1:T(8,128)S(1)} fusion(f32[512,64]{0,1:T(8,128)S(1)} %copy-done, f32[512,512]{1,0:T(8,128)} %param.6, bf16[512,512]{1,0:T(8,128)(2,1)} %param.7), kind=kOutput, calls=%fused_computation.8 | convolution fusion | flops 201850880 | bytes 1835008 | tf_op jit(solution)/shard_map/dot_general | solution.py:16
  4.1 24.7 %all_to_all.25 = f32[32,8,128]{2,1,0:T(8,128)S(1)} all-to-all(f32[32,8,128]{2,1,0:T(8,128)S(1)} %bitcast.93), channel_id=1, replica_groups=mesh['far'=8,'near'=4,'x'=4,'y'=4,'core'=2] {'x','y','core'}, dimensions={0} | all-to-all | bytes 262144 | tf_op jit(solution)/shard_map/all_to_all | solution.py:38
  28.8 0.7 broadcast_in_dim.6
  29.5 3.9 %all-to-all-start.1 = ((f32[32,8,128]{2,1,0:T(8,128)}), f32[32,8,128]{2,1,0:T(8,128)S(1)}, u32[]{:S(2)}, u32[]{:S(2)}) async-start(f32[32,8,128]{2,1,0:T(8,128)} %broadcast_in_dim.6), calls=%async_computation.1 | async-start | bytes 262144 | tf_op jit(solution)/shard_map/all_to_all | solution.py:38
  33.4 1.1 fusion.3
  34.5 1.6 copy.19
  36.1 5.1 %all-to-all-done.1 = f32[32,8,128]{2,1,0:T(8,128)S(1)} async-done(((f32[32,8,128]{2,1,0:T(8,128)}), f32[32,8,128]{2,1,0:T(8,128)S(1)}, u32[]{:S(2)}, u32[]{:S(2)}) %all-to-all-start.1) | async-done | bytes 131104 | tf_op jit(solution)/shard_map/all_to_all | solution.py:38
  41.2 0.3 fusion.27
  41.4 1.1 fusion.26
  42.6 0.1 maximum_maximum_fusion
  42.6 8.4 %all_to_all.26 = f32[4,72,128]{2,1,0:T(8,128)S(1)} all-to-all(f32[4,72,128]{2,1,0:T(8,128)S(1)} %bitcast.92), channel_id=1, replica_groups=mesh['far'=8,'near'=4,'x'=4,'y'=4,'core'=2] {'near'}, dimensions={0} | all-to-all | bytes 294912 | tf_op jit(solution)/shard_map/all_to_all | solution.py:38
  51.1 42.3 %psum.7 = f32[72,128]{1,0:T(8,128)S(1)} all-reduce(f32[72,128]{1,0:T(8,128)S(1)} %reduce_sum.37), channel_id=1, replica_groups=mesh['far'=8,'near'=4,'x'=4,'y'=4,'core'=2] {'far'}, use_global_device_ids=true, to_apply=%region_2.0 | all-reduce | flops 9216 | bytes 73728 | tf_op jit(solution)/shard_map/psum | solution.py:65
  93.4 8.7 %all_to_all.27 = f32[4,72,128]{2,1,0:T(8,128)S(1)} all-to-all(f32[4,72,128]{2,1,0:T(8,128)S(1)} %broadcast_in_dim.7), channel_id=1, replica_groups=mesh['far'=8,'near'=4,'x'=4,'y'=4,'core'=2] {'near'}, dimensions={0} | all-to-all | bytes 294912 | tf_op jit(solution)/shard_map/all_to_all | solution.py:38
  102.1 0.1 fusion.24
  102.2 0.1 copy.14
  102.3 0.1 copy.15
  102.3 5.8 %cholesky.44 = f32[64,64]{1,0:T(8,128)S(1)} custom-call(f32[64,64]{1,0:T(8,128)S(1)} %fusion.15), custom_call_target="Cholesky" | custom-call | tf_op jit(solution)/shard_map/jit(cholesky)/cholesky | solution.py:47
  108.2 0.6 compare_reduce_fusion.1
  108.9 1.3 fusion.22
  110.1 4.9 %custom-call.6 = f32[1,64,64]{1,2,0:T(8,128)S(1)} custom-call(f32[1,64,64]{2,1,0:T(8,128)S(1)} %get-tuple-element.10), custom_call_target="InvertDiagBlocksLowerTriangular" | custom-call | tf_op jit(solution)/shard_map/triangular_solve/custom-call.0 | solution.py:48
  115.0 0.3 fusion.7
  115.3 0.3 fusion.28
  115.6 0.3 fusion.29
  115.8 0.3 fusion.31
  116.1 0.3 fusion.30
  116.4 0.1 pad_maximum_fusion.1
  116.4 1.1 broadcast_in_dim.8
  117.5 12.8 %all-to-all-start.4 = ((f32[32,64,128]{2,1,0:T(8,128)}), f32[32,64,128]{2,1,0:T(8,128)S(1)}, u32[]{:S(2)}, u32[]{:S(2)}) async-start(f32[32,64,128]{2,1,0:T(8,128)} %broadcast_in_dim.8), calls=%async_computation.4 | async-start | bytes 2097152 | tf_op jit(solution)/shard_map/all_to_all | solution.py:38
  130.4 0.3 fusion.32
  130.7 16.7 %all-to-all-done.4 = f32[32,64,128]{2,1,0:T(8,128)S(1)} async-done(((f32[32,64,128]{2,1,0:T(8,128)}), f32[32,64,128]{2,1,0:T(8,128)S(1)}, u32[]{:S(2)}, u32[]{:S(2)}) %all-to-all-start.4) | async-done | bytes 1048608 | tf_op jit(solution)/shard_map/all_to_all | solution.py:38
  147.4 0.1 reduce_sum.38
  147.5 0.1 copy.16
  147.6 0.1 copy.17
  147.7 5.8 %cholesky.55 = f32[64,64]{1,0:T(8,128)S(1)} custom-call(f32[64,64]{1,0:T(8,128)S(1)} %fusion.12), custom_call_target="Cholesky" | custom-call | tf_op jit(solution)/shard_map/jit(cholesky)/cholesky | solution.py:47
  153.5 0.6 compare_reduce_fusion
  154.2 0.7 fusion.9
  154.8 4.9 %custom-call.7 = f32[1,64,64]{1,2,0:T(8,128)S(1)} custom-call(f32[1,64,64]{2,1,0:T(8,128)S(1)} %fusion.9), custom_call_target="InvertDiagBlocksLowerTriangular" | custom-call | tf_op jit(solution)/shard_map/triangular_solve/custom-call.0 | solution.py:48
  159.7 0.2 fusion.5
  160.0 0.3 fusion.2
  160.3 0.3 fusion.34
  160.6 0.3 fusion.33
  161.0 0.0 copy-start.3
  161.0 0.7 fusion.23
  161.7 1.8 %fusion.1 = bf16[512,512]{1,0:T(8,128)(2,1)} fusion(f32[64,512]{1,0:T(8,128)S(1)} %fusion.33, f32[64,512]{1,0:T(8,128)S(1)} %fusion.34, f32[64]{0:T(128)S(1)} %sqrt_add_fusion), kind=kOutput, calls=%fused_computation.3 | convolution fusion | flops 201883648 | bytes 786688 | tf_op jit(solution)/shard_map/dot_general | solution.py:16
  163.6 2.1 %fusion = f32[512,512]{1,0:T(8,128)} fusion(f32[64,512]{1,0:T(8,128)S(1)} %fusion.33, f32[64,512]{1,0:T(8,128)S(1)} %fusion.34, f32[512,512]{1,0:T(8,128)S(1)} %copy-done.1, bf16[512,512]{1,0:T(8,128)(2,1)S(1)} %copy-done.2), kind=kOutput, calls=%fused_computation.2 | convolution fusion | flops 202375168 | bytes 2883584 | tf_op jit(solution)/shard_map/dot_general | solution.py:16
  (17 shorter events, 0.2 us)
Async XLA Ops:
  0.6 0.9 copy-start
  0.6 32.7 %copy-start.1 = (f32[512,512]{1,0:T(8,128)S(1)}, f32[512,512]{1,0:T(8,128)}, u32[]{:S(2)}) copy-start(f32[512,512]{1,0:T(8,128)} %param.6) | copy-start | bytes 3145732
  4.1 29.3 %copy-start.2 = (bf16[512,512]{1,0:T(8,128)(2,1)S(1)}, bf16[512,512]{1,0:T(8,128)(2,1)}, u32[]{:S(2)}) copy-start(bf16[512,512]{1,0:T(8,128)(2,1)} %param.7) | copy-start | bytes 1572868
  29.5 11.7 %all-to-all-start.1 = ((f32[32,8,128]{2,1,0:T(8,128)}), f32[32,8,128]{2,1,0:T(8,128)S(1)}, u32[]{:S(2)}, u32[]{:S(2)}) async-start(f32[32,8,128]{2,1,0:T(8,128)} %broadcast_in_dim.6), calls=%async_computation.1 | async-start | bytes 262144 | tf_op jit(solution)/shard_map/all_to_all | solution.py:38
  117.5 29.9 %all-to-all-start.4 = ((f32[32,64,128]{2,1,0:T(8,128)}), f32[32,64,128]{2,1,0:T(8,128)S(1)}, u32[]{:S(2)}, u32[]{:S(2)}) async-start(f32[32,64,128]{2,1,0:T(8,128)} %broadcast_in_dim.8), calls=%async_computation.4 | async-start | bytes 2097152 | tf_op jit(solution)/shard_map/all_to_all | solution.py:38
  161.0 2.6 %copy-start.3 = (f32[64,512]{1,0:T(8,128)}, f32[64,512]{1,0:T(8,128)S(1)}, u32[]{:S(2)}) copy-start(f32[64,512]{1,0:T(8,128)S(1)} %fusion.33) | copy-start | bytes 393220

commit v2 on v1

v2 whole, which is shorter than its diff:
```python
import functools
import math

import jax
import jax.numpy as jnp
from jax import lax
from jax.experimental import pallas as pl
from jax.experimental.pallas import tpu as pltpu
from jax.sharding import Mesh, PartitionSpec as P

NROW = 16384
NCOL = 16384
RANK = 64
HIGH = lax.Precision.HIGHEST
COL = ("x", "y", "core")
NEAR = ("near",)
FAR = ("far",)
SIDE = 512
F32 = jnp.float32


def dot(a, b, dims):
    return lax.dot_general(
        a, b, (dims, ((), ())), precision=HIGH, preferred_element_type=F32
    )


def nn(a, b):
    return dot(a, b, ((1,), (0,)))


def nt(a, b):
    return dot(a, b, ((1,), (1,)))


def tn(a, b):
    return dot(a, b, ((0,), (0,)))


def call(kernel, outs, *args):
    whole = pl.BlockSpec(memory_space=pltpu.VMEM)
    return pl.pallas_call(
        kernel,
        out_shape=[jax.ShapeDtypeStruct(s, d) for s, d in outs],
        in_specs=[whole] * len(args),
        out_specs=[whole] * len(outs),
        name=kernel.__name__,
    )(*args)


def write_tiles(ref, a):
    for i in range(8):
        for j in range(4):
            ref[4 * i + j] = a[8 * i : 8 * i + 8, 128 * j : 128 * j + 128]


def read_tiles(ref):
    rows = [jnp.concatenate([ref[4 * i + j] for j in range(4)], axis=1) for i in range(8)]
    return jnp.concatenate(rows, axis=0)


def places(shape):
    return lax.broadcasted_iota(jnp.int32, shape, 0), lax.broadcasted_iota(jnp.int32, shape, 1)


def fold(a):
    return jnp.concatenate([a[:32], a[32:]], axis=1)


def unfold(a):
    return jnp.concatenate([a[:, :64], a[:, 64:]], axis=0)


def factor(gram):
    row, lane = places((RANK, RANK))
    eye = jnp.where(row == lane, 1.0, 0.0).astype(F32)
    both = jnp.concatenate([gram, eye], axis=1)
    blocks = [both[8 * b : 8 * b + 8] for b in range(8)]
    in_block, _ = places((8, 128))
    for k in range(RANK - 1):
        at, r = divmod(k, 8)
        line = blocks[at][r : r + 1]
        line = line / line[:, k : k + 1]
        for b in range(at, 8):
            column = blocks[b][:, k : k + 1]
            if b == at:
                if r == 7:
                    continue
                column = jnp.where(in_block > r, column, 0.0)
            blocks[b] = blocks[b] - column * line
    both = jnp.concatenate(blocks, axis=0)
    upper, inverse = both[:, :64], both[:, 64:]
    pivot = jnp.sum(jnp.where(row == lane, upper, 0.0), axis=1, keepdims=True)
    root = 1.0 / jnp.sqrt(pivot)
    upper = jnp.where(row <= lane, upper * root, 0.0)
    return upper, inverse * root


def left_part(momentum, gradient, factor_t, part):
    blended = momentum[...] + gradient[...].astype(F32)
    write_tiles(part, nt(factor_t[...], blended))


def left_tile(parts, copies):
    tile = jnp.sum(parts[...], axis=0)
    for i in range(32):
        copies[i] = tile


def right_part(tiles, momentum, gradient, send):
    left_raw = read_tiles(tiles)
    blended = momentum[...] + gradient[...].astype(F32)
    write_tiles(send, nn(left_raw, blended))
    gram = fold(nt(left_raw, left_raw))
    for i in range(4):
        send[32 + i] = gram[8 * i : 8 * i + 8]


def first_pass(total, factor_t, upper_one, inverse_one, right_one, copies):
    gram = unfold(jnp.concatenate([total[32 + i] for i in range(4)], axis=0))
    upper, inverse = factor(gram)
    upper_one[...] = upper
    inverse_one[...] = inverse
    right = nn(inverse, read_tiles(total))
    right_one[...] = right
    gram_two = nt(nn(inverse, factor_t[...]), right)
    squared = nt(right, right)
    row, lane = places((RANK, RANK))
    diagonal = jnp.sum(jnp.where(row == lane, squared, 0.0), axis=0, keepdims=True)
    pair = fold(jnp.where(row <= lane, gram_two, squared))
    last = jnp.concatenate([diagonal, jnp.zeros((1, 64), F32)], axis=1)
    last = jnp.broadcast_to(last, (8, 128))
    for i in range(32):
        copies[i, :32] = pair
        copies[i, 32:] = last


def second_pass(
    pairs, tiles, inverse_one, right_one, momentum, gradient,
    update, left, normed, new_momentum,
):
    pair = jnp.sum(pairs[...], axis=0)
    mixed = unfold(pair[:32])
    diagonal = pair[32:33, :64]
    row, lane = places((RANK, RANK))
    flipped = mixed.T
    gram_two = jnp.where(row <= lane, mixed, flipped)
    squared = jnp.where(row > lane, mixed, flipped)
    squared = jnp.where(row == lane, diagonal, squared)
    _, inverse = factor(gram_two)
    left_t = nn(inverse, nn(inverse_one[...], read_tiles(tiles)))
    right_t = nn(inverse, right_one[...])
    squares = jnp.sum(nn(inverse, squared) * inverse, axis=1, keepdims=True)
    normed_t = right_t / (jnp.sqrt(squares) + 1e-06)
    left[...] = left_t
    normed[...] = normed_t
    scale = math.sqrt(NROW * NCOL / RANK)
    update[...] = (scale * tn(left_t, normed_t)).astype(jnp.bfloat16)
    blended = momentum[...] + gradient[...].astype(F32)
    new_momentum[...] = blended - 0.05 * tn(left_t, right_t)


def exchange(chunks, axes):
    return lax.all_to_all(chunks, axes, 0, 0, tiled=True)


def on_device(momentum, gradient, right_factor):
    factor_t = right_factor.T
    flat = (RANK, SIDE)
    square = (RANK, RANK)
    (part,) = call(left_part, [((32, 8, 128), F32)], momentum, gradient, factor_t)
    (copies,) = call(left_tile, [((32, 8, 128), F32)], exchange(part, COL))
    tiles = exchange(copies, COL)
    (send,) = call(right_part, [((36, 8, 128), F32)], tiles, momentum, gradient)
    near = jnp.sum(exchange(send.reshape(4, 72, 128), NEAR), axis=0)
    far = lax.psum(near, FAR)
    total = exchange(jnp.broadcast_to(far[None], (4, 72, 128)), NEAR).reshape(36, 8, 128)
    upper_one, inverse_one, right_one, copies = call(
        first_pass,
        [(square, F32), (square, F32), (flat, F32), ((32, 40, 128), F32)],
        total,
        factor_t,
    )
    first_factor = upper_one.T / jnp.sqrt(F32(NROW) * F32(NCOL))
    pairs = exchange(copies, COL)
    full = (SIDE, SIDE)
    update, left_t, normed_t, new_momentum = call(
        second_pass,
        [(full, jnp.bfloat16), (flat, F32), (flat, F32), (full, F32)],
        pairs, tiles, inverse_one, right_one, momentum, gradient,
    )
    return (update, left_t.T, normed_t.T, new_momentum, first_factor)


def solution(mesh):
    inner = Mesh(mesh.devices.reshape(8, 4, 4, 4, 2), FAR + NEAR + COL)
    row, col = FAR + NEAR, COL
    in_specs = (P(row, col), P(row, col), P(col, None))
    out_specs = (P(row, col), P(row, None), P(col, None), P(row, col), P())
    return jax.shard_map(
        on_device, mesh=inner, in_specs=in_specs, out_specs=out_specs, check_vma=False
    )
```

time: 166 us -> 152 us (0.916)
  other arithmetic: 27 us -> 0.02 us
  Pallas kernels: 0 us -> 26.2 us
  blocking collectives: 84 us -> 97.6 us
  matrix products: 10.6 us -> 0 us
  waiting for transfers between devices: 21.8 us -> 12.3 us
  starting transfers between devices: 16.8 us -> 13.1 us
  local copies, waits for them, and re-layouts: 4.62 us -> 1.56 us
    pallas_call x0 -> x5, Pallas kernels: none -> 26.2 us  [call(): pl.pallas_call(kernel, out_shape=[jax.ShapeDtypeStruct(s, d) for s, d in...]
    another operation x9 -> x0, other arithmetic: 23.5 us -> none  [the longest x6 13 us: lower_and_inverse(): lower = jnp.linalg.cholesky(gram)]
    all_to_all x3 -> x4, blocking collectives: 41.7 us -> 56.8 us  [exchange(): return lax.all_to_all(chunks, axes, 0, 0, tiled=True)]
    dot_general x13 -> x0, matrix products: 10.1 us -> none  [dot(): lax.dot_general(a, b, (dims, ((), ())), precision=HIGH, preferred_element...]
    all_to_all x2 -> x1, waiting for transfers between devices: 21.8 us -> 12.3 us  [exchange(): return lax.all_to_all(chunks, axes, 0, 0, tiled=True)]
    all_to_all x2 -> x1, starting transfers between devices: 16.8 us -> 13.1 us  [exchange(): return lax.all_to_all(chunks, axes, 0, 0, tiled=True)]
    div x6 -> x1, other arithmetic: 2.06 us -> 0.01 us  [on_device(): first_factor = upper_one.T / jnp.sqrt(F32(NROW) * F32(NCOL))]
    broadcast_in_dim x3 -> x1, local copies, waits for them, and re-layouts: 1.77 us -> 0.01 us  [on_device(): jnp.broadcast_to(far[None], (4, 72, 128))]
  transfers between devices with their start and end apart: 2 -> 1, of which waited for: 2 -> 1; matrix products, arithmetic and copies ran while one was open for 2% -> 0% of each run, Pallas kernels for 0% -> 0%
where the time goes in v2:
time: 152 us; the launch traced here: 151 us
  blocking collectives  97.6 us (64%)
  Pallas kernels  26.2 us (17%)
  starting transfers between devices  13.1 us (9%)
  waiting for transfers between devices  12.3 us (8%)
  local copies, waits for them, and re-layouts  1.56 us (1%)
    all_to_all x4, blocking collectives, exchange(): return lax.all_to_all(chunks, axes, 0, 0, tiled=True)  56.8 us
    psum x1, blocking collectives, on_device(): far = lax.psum(near, FAR)  40.8 us
    pallas_call x5, Pallas kernels, call(): pl.pallas_call(kernel, out_shape=[jax.ShapeDtypeStruct(s, d) for s, d in...  26.2 us
    all_to_all x1, starting transfers between devices, exchange(): return lax.all_to_all(chunks, axes, 0, 0, tiled=True)  13.1 us
    all_to_all x1, waiting for transfers between devices, exchange(): return lax.all_to_all(chunks, axes, 0, 0, tiled=True)  12.3 us
  transfers between devices with their start and end apart: 1, of which 1 were waited for; matrix products, arithmetic and copies ran while one was open for 0% of the time, Pallas kernels for 0%

profile of v2, /device:TPU:1, one launch (start us, length us, event | category | flops | bytes accessed | tf_op | source)
XLA Modules:
  0.0 151.3 jit_solution(16127689317992008241)
XLA Ops:
  0.6 3.1 %left_part.1 = f32[32,8,128]{2,1,0:T(8,128)} custom-call(f32[512,512]{1,0:T(8,128)} %momentum.5, bf16[512,512]{1,0:T(8,128)(2,1)} %gradient.5, f32[64,512]{1,0:T(8,128)} %bitcast.9), custom_call_target="tpu_custom_call" | custom-call | tf_op jit(solution)/shard_map/left_part/pallas_call | solution.py:42
  3.8 26.1 %all_to_all.25.parts = f32[32,8,128]{2,1,0:T(8,128)} all-to-all(f32[32,8,128]{2,1,0:T(8,128)} %left_part.1), channel_id=1, replica_groups=mesh['far'=8,'near'=4,'x'=4,'y'=4,'core'=2] {'x','y','core'}, dimensions={0} | all-to-all | bytes 262144 | tf_op jit(solution)/shard_map/all_to_all | solution.py:164
  29.8 1.6 %left_tile.1 = f32[32,8,128]{2,1,0:T(8,128)} custom-call(f32[32,8,128]{2,1,0:T(8,128)} %all_to_all.25.parts), custom_call_target="tpu_custom_call" | custom-call | tf_op jit(solution)/shard_map/left_tile/pallas_call | solution.py:42
  31.4 12.4 %all_to_all.26.tiles = f32[32,8,128]{2,1,0:T(8,128)} all-to-all(f32[32,8,128]{2,1,0:T(8,128)} %left_tile.1), channel_id=1, replica_groups=mesh['far'=8,'near'=4,'x'=4,'y'=4,'core'=2] {'x','y','core'}, dimensions={0} | all-to-all | bytes 262144 | tf_op jit(solution)/shard_map/all_to_all | solution.py:164
  43.8 2.9 %right_part.1 = f32[36,8,128]{2,1,0:T(8,128)} custom-call(f32[32,8,128]{2,1,0:T(8,128)} %all_to_all.26.tiles, f32[512,512]{1,0:T(8,128)} %momentum.5, bf16[512,512]{1,0:T(8,128)(2,1)} %gradient.5), custom_call_target="tpu_custom_call" | custom-call | tf_op jit(solution)/shard_map/right_part/pallas_call | solution.py:42
  46.7 9.4 %all_to_all.27 = f32[4,72,128]{2,1,0:T(8,128)S(1)} all-to-all(f32[4,72,128]{2,1,0:T(8,128)} %bitcast.7), channel_id=1, replica_groups=mesh['far'=8,'near'=4,'x'=4,'y'=4,'core'=2] {'near'}, dimensions={0} | all-to-all | bytes 294912 | tf_op jit(solution)/shard_map/all_to_all | solution.py:164
  56.1 40.8 %psum.7 = f32[72,128]{1,0:T(8,128)S(1)} all-reduce(f32[72,128]{1,0:T(8,128)S(1)} %reduce_sum.9), channel_id=1, replica_groups=mesh['far'=8,'near'=4,'x'=4,'y'=4,'core'=2] {'far'}, use_global_device_ids=true, to_apply=%region_1.0 | all-reduce | flops 9216 | bytes 73728 | tf_op jit(solution)/shard_map/psum | solution.py:176
  96.9 9.0 %all_to_all.28 = f32[4,72,128]{2,1,0:T(8,128)} all-to-all(f32[4,72,128]{2,1,0:T(8,128)S(1)} %broadcast_in_dim.2), channel_id=1, replica_groups=mesh['far'=8,'near'=4,'x'=4,'y'=4,'core'=2] {'near'}, dimensions={0} | all-to-all | bytes 294912 | tf_op jit(solution)/shard_map/all_to_all | solution.py:164
  105.9 8.0 %first_pass.1 = (f32[64,64]{1,0:T(8,128)}, f32[64,64]{1,0:T(8,128)}, f32[64,512]{1,0:T(8,128)}, f32[32,40,128]{2,1,0:T(8,128)}) custom-call(f32[36,8,128]{2,1,0:T(8,128)} %bitcast.8, f32[64,512]{1,0:T(8,128)} %bitcast.10), custom_call_target="tpu_custom_call" | custom-call | tf_op jit(solution)/shard_map/first_pass/pallas_call | solution.py:42
  113.9 0.0 copy-start.1
  113.9 13.1 %all-to-all-start.4 = ((f32[32,40,128]{2,1,0:T(8,128)}), f32[32,40,128]{2,1,0:T(8,128)S(1)}, u32[]{:S(2)}, u32[]{:S(2)}) async-start(f32[32,40,128]{2,1,0:T(8,128)} %get-tuple-element.13), calls=%async_computation.4 | async-start | bytes 1310720 | tf_op jit(solution)/shard_map/all_to_all | solution.py:164
  126.9 0.0 copy-done.1
  127.0 0.7 copy.8
  127.7 12.3 %all-to-all-done.4.pairs = f32[32,40,128]{2,1,0:T(8,128)S(1)} async-done(((f32[32,40,128]{2,1,0:T(8,128)}), f32[32,40,128]{2,1,0:T(8,128)S(1)}, u32[]{:S(2)}, u32[]{:S(2)}) %all-to-all-start.4) | async-done | bytes 655392 | tf_op jit(solution)/shard_map/all_to_all | solution.py:164
  140.0 0.0 copy-start
  140.0 0.8 copy-done
  140.8 10.5 %second_pass.1 = (bf16[512,512]{1,0:T(8,128)(2,1)}, f32[64,512]{1,0:T(8,128)}, f32[64,512]{1,0:T(8,128)}, f32[512,512]{1,0:T(8,128)}) custom-call(f32[32,40,128]{2,1,0:T(8,128)} %copy-done, f32[32,8,128]{2,1,0:T(8,128)} %all_to_all.26.tiles, f32[64,64]{1,0:T(8,128)} %get-tuple-element.14.inverse_one, f32[64,512]{1,0:T(8,128)} %get-tuple-element.15.right_one, ...), custom_call_target="tpu_custom_call" | custom-call | tf_op jit(solution)/shard_map/second_pass/pallas_call | solution.py:42
  (3 shorter events, 0.0 us)
Async XLA Ops:
  113.9 13.1 %copy-start.1 = (f32[64,64]{1,0:T(8,128)S(1)}, f32[64,64]{1,0:T(8,128)}, u32[]{:S(2)}) copy-start(f32[64,64]{1,0:T(8,128)} %get-tuple-element.20) | copy-start | bytes 49156
  113.9 26.1 %all-to-all-start.4 = ((f32[32,40,128]{2,1,0:T(8,128)}), f32[32,40,128]{2,1,0:T(8,128)S(1)}, u32[]{:S(2)}, u32[]{:S(2)}) async-start(f32[32,40,128]{2,1,0:T(8,128)} %get-tuple-element.13), calls=%async_computation.4 | async-start | bytes 1310720 | tf_op jit(solution)/shard_map/all_to_all | solution.py:164
  140.0 0.8 copy-start

commit v3 on v2

v3 whole, which is shorter than its diff:
```python
import math

import jax
import jax.numpy as jnp
from jax import lax
from jax.experimental import pallas as pl
from jax.experimental.pallas import tpu as pltpu
from jax.sharding import Mesh, PartitionSpec as P

NROW = 16384
NCOL = 16384
RANK = 64
HIGH = lax.Precision.HIGHEST
COL = ("x", "y", "core")
NEAR = ("near",)
FAR = ("far",)
SIDE = 512
F32 = jnp.float32


def dot(a, b, dims):
    return lax.dot_general(
        a, b, (dims, ((), ())), precision=HIGH, preferred_element_type=F32
    )


def nn(a, b):
    return dot(a, b, ((1,), (0,)))


def nt(a, b):
    return dot(a, b, ((1,), (1,)))


def tn(a, b):
    return dot(a, b, ((0,), (0,)))


ANY = pl.BlockSpec(memory_space=pl.ANY)
VMEM = pl.BlockSpec(memory_space=pltpu.VMEM)


def call(kernel, outs, *args, far_in=(), far_out=(), scratch=()):
    args = [
        a if i in far_in else pltpu.with_memory_space_constraint(a, pltpu.VMEM)
        for i, a in enumerate(args)
    ]
    return pl.pallas_call(
        kernel,
        out_shape=[
            jax.ShapeDtypeStruct(s, d) if i in far_out else pltpu.VMEM(s, d)
            for i, (s, d) in enumerate(outs)
        ],
        in_specs=[ANY if i in far_in else VMEM for i in range(len(args))],
        out_specs=[ANY if i in far_out else VMEM for i in range(len(outs))],
        scratch_shapes=list(scratch),
        name=kernel.__name__,
    )(*args)


def write_tiles(ref, a):
    for i in range(8):
        for j in range(4):
            ref[4 * i + j] = a[8 * i : 8 * i + 8, 128 * j : 128 * j + 128]


def read_tiles(ref):
    rows = [jnp.concatenate([ref[4 * i + j] for j in range(4)], axis=1) for i in range(8)]
    return jnp.concatenate(rows, axis=0)


def places(shape):
    return lax.broadcasted_iota(jnp.int32, shape, 0), lax.broadcasted_iota(jnp.int32, shape, 1)


def fold(a):
    return jnp.concatenate([a[:32], a[32:]], axis=1)


def unfold(a):
    return jnp.concatenate([a[:, :64], a[:, 64:]], axis=0)


def factor(gram, width=8):
    row, lane = places((RANK, RANK))
    eye = jnp.where(row == lane, 1.0, 0.0).astype(F32)
    both = jnp.concatenate([gram, eye], axis=1)
    blocks = [both[8 * b : 8 * b + 8] for b in range(8)]
    in_block, _ = places((8, 128))
    for k in range(0, RANK, width):
        at, r = divmod(k, 8)
        columns = [
            {b: jnp.broadcast_to(blocks[b][:, k + j : k + j + 1], (8, 128)) for b in range(at, 8)}
            for j in range(width)
        ]
        lines = [blocks[at][r + j : r + j + 1] for j in range(width)]
        scaled = []
        for j in range(width):
            over = 1.0 / columns[j][at][r + j : r + j + 1]
            scaled.append(lines[j] * over)
            for l in range(j + 1, width):
                share = columns[j][at][r + l : r + l + 1] * over
                lines[l] = lines[l] - share * lines[j]
                for b in range(at, 8):
                    columns[l][b] = columns[l][b] - columns[j][b] * share
        for b in range(at, 8):
            new = blocks[b]
            for j in range(width):
                new = new - columns[j][b] * scaled[j]
            if b == at:
                new = jnp.where(in_block >= r + width, new, blocks[b])
                for j in range(width):
                    new = jnp.where(in_block == r + j, lines[j], new)
            blocks[b] = new
    both = jnp.concatenate(blocks, axis=0)
    upper, inverse = both[:, :64], both[:, 64:]
    pivot = jnp.sum(jnp.where(row == lane, upper, 0.0), axis=1, keepdims=True)
    root = 1.0 / jnp.sqrt(pivot)
    upper = jnp.where(row <= lane, upper * root, 0.0)
    return upper, inverse * root


STEPS = 4
STEP = SIDE // STEPS


def rows_of(i):
    return pl.ds(STEP * i, STEP)


def left_part(momentum, gradient, factor_t, part, blended, old, change, sems):
    copies = [
        pltpu.make_async_copy(momentum, old, sems.at[0]),
        pltpu.make_async_copy(gradient, change, sems.at[1]),
    ]
    for copy in copies:
        copy.start()
    for copy in copies:
        copy.wait()
    block = old[...] + change[...].astype(F32)
    blended[...] = block
    write_tiles(part, nt(factor_t[...], block))


def left_tile(parts, copies):
    tile = jnp.sum(parts[...], axis=0)
    for i in range(32):
        copies[i] = tile


def right_part(tiles, blended, send):
    left_raw = read_tiles(tiles)
    product = nn(left_raw, blended[...])
    gram = fold(nt(left_raw, left_raw))
    for i in range(8):
        for j in range(4):
            tile = product[8 * i : 8 * i + 8, 128 * j : 128 * j + 128]
            send[i // 2, 32 * (i % 2) + 8 * j : 32 * (i % 2) + 8 * j + 8] = tile
    for i in range(4):
        send[i, 64:] = gram


def first_factor_of(gram, upper_one, inverse_one):
    upper, inverse = factor(unfold(gram[...]))
    upper_one[...] = upper
    inverse_one[...] = inverse


def second_gram(total, inverse_one, factor_t, right_one, copies):
    inverse = inverse_one[...]
    right = nn(inverse, read_tiles(total))
    right_one[...] = right
    gram_two = nt(nn(inverse, factor_t[...]), right)
    squared = nt(right, right)
    row, lane = places((RANK, RANK))
    diagonal = jnp.sum(jnp.where(row == lane, squared, 0.0), axis=0, keepdims=True)
    pair = fold(jnp.where(row <= lane, gram_two, squared))
    last = jnp.concatenate([diagonal, jnp.zeros((1, 64), F32)], axis=1)
    last = jnp.broadcast_to(last, (8, 128))
    for i in range(32):
        copies[i, :32] = pair
        copies[i, 32:] = last


def left_once(tiles, inverse_one, left_one):
    left_one[...] = nn(inverse_one[...], read_tiles(tiles))


def halves(a):
    high = a.astype(jnp.bfloat16)
    return high, (a - high.astype(F32)).astype(jnp.bfloat16)


def results(
    pairs, left_one, right_one, blended,
    update, left, normed, new_momentum, u, l, n, m, sems,
):
    pair = jnp.sum(pairs[...], axis=0)
    mixed = unfold(pair[:32])
    diagonal = pair[32:33, :64]
    row, lane = places((RANK, RANK))
    flipped = mixed.T
    gram_two = jnp.where(row <= lane, mixed, flipped)
    squared = jnp.where(row > lane, mixed, flipped)
    squared = jnp.where(row == lane, diagonal, squared)
    _, inverse = factor(gram_two)
    squares = jnp.sum(nn(inverse, squared) * inverse, axis=1, keepdims=True)
    left_t = nn(inverse, left_one[...])
    right_t = nn(inverse, right_one[...])
    normed_t = right_t / (jnp.sqrt(squares) + 1e-06)
    l[...] = left_t
    n[...] = normed_t
    copies = [
        pltpu.make_async_copy(l, left, sems.at[0, 0]),
        pltpu.make_async_copy(n, normed, sems.at[0, 1]),
    ]
    for copy in copies:
        copy.start()
    high, low = halves(left_t)
    lefts = jnp.concatenate([high, high, low], axis=0)
    high, low = halves(0.05 * right_t)
    rights = jnp.concatenate([high, low, high], axis=0)
    high, low = halves(math.sqrt(NROW * NCOL / RANK) * normed_t)
    norms = jnp.concatenate([high, low, high], axis=0)

    def product(i, other):
        part = lefts[:, STEP * i : STEP * i + STEP]
        return lax.dot_general(
            part, other, (((0,), (0,)), ((), ())), preferred_element_type=F32
        )

    for i in range(STEPS):
        m[rows_of(i)] = blended[rows_of(i)] - product(i, rights)
        u[rows_of(i)] = product(i, norms).astype(jnp.bfloat16)
        for k, (source, target) in enumerate(((m, new_momentum), (u, update))):
            copy = pltpu.make_async_copy(
                source.at[rows_of(i)], target.at[rows_of(i)], sems.at[1 + i, k]
            )
            copy.start()
            copies.append(copy)
    for copy in copies:
        copy.wait()


def exchange(chunks, axes):
    return lax.all_to_all(chunks, axes, 0, 0, tiled=True)


def on_device(momentum, gradient, right_factor):
    factor_t = right_factor.T
    flat, square, full = (RANK, SIDE), (RANK, RANK), (SIDE, SIDE)
    tiled = ((32, 8, 128), F32)
    part, blended = call(
        left_part,
        [tiled, (full, F32)],
        momentum, gradient, factor_t,
        far_in=(0, 1),
        scratch=[
            pltpu.VMEM(full, F32),
            pltpu.VMEM(full, jnp.bfloat16),
            pltpu.SemaphoreType.DMA((2,)),
        ],
    )
    (copies,) = call(left_tile, [tiled], exchange(part, COL))
    tiles = exchange(copies, COL)
    (send,) = call(right_part, [((4, 96, 128), F32)], tiles, blended)
    near = jnp.sum(exchange(send, NEAR), axis=0)
    far = lax.psum(near, FAR)
    quarters = jnp.broadcast_to(far[None, :64], (4, 64, 128))
    total = exchange(quarters, NEAR).reshape(32, 8, 128)
    upper_one, inverse_one = call(
        first_factor_of, [(square, F32), (square, F32)], far[64:]
    )
    first_factor = upper_one.T / jnp.sqrt(F32(NROW) * F32(NCOL))
    right_one, copies = call(
        second_gram, [(flat, F32), ((32, 40, 128), F32)], total, inverse_one, factor_t
    )
    pairs = exchange(copies, COL)
    (left_one,) = call(left_once, [(flat, F32)], tiles, inverse_one)
    update, left_t, normed_t, new_momentum = call(
        results,
        [(full, jnp.bfloat16), (flat, F32), (flat, F32), (full, F32)],
        pairs, left_one, right_one, blended,
        far_out=(0, 1, 2, 3),
        scratch=[
            pltpu.VMEM(full, jnp.bfloat16),
            pltpu.VMEM(flat, F32),
            pltpu.VMEM(flat, F32),
            pltpu.VMEM(full, F32),
            pltpu.SemaphoreType.DMA((1 + STEPS, 2)),
        ],
    )
    return (update, left_t.T, normed_t.T, new_momentum, first_factor)


def solution(mesh):
    inner = Mesh(mesh.devices.reshape(8, 4, 4, 4, 2), FAR + NEAR + COL)
    row, col = FAR + NEAR, COL
    in_specs = (P(row, col), P(row, col), P(col, None))
    out_specs = (P(row, col), P(row, None), P(col, None), P(row, col), P())
    return jax.shard_map(
        on_device, mesh=inner, in_specs=in_specs, out_specs=out_specs, check_vma=False
    )
```

time: 152 us -> 133 us (0.88)
  Pallas kernels: 26.2 us -> 10.6 us
  blocking collectives: 97.6 us -> 86.5 us
  starting transfers between devices: 13.1 us -> 17.7 us
  waiting for transfers between devices: 12.3 us -> 15.1 us
    pallas_call x5 -> x7, Pallas kernels: 26.2 us -> 10.6 us  [call(): pl.pallas_call(kernel, out_shape=[jax.ShapeDtypeStruct(s, d) if i in far_...]
    all_to_all x4 -> x3, blocking collectives: 56.8 us -> 44.4 us  [exchange(): return lax.all_to_all(chunks, axes, 0, 0, tiled=True)]
    all_to_all x1 -> x2, starting transfers between devices: 13.1 us -> 17.7 us  [exchange(): return lax.all_to_all(chunks, axes, 0, 0, tiled=True)]
    all_to_all x1 -> x2, waiting for transfers between devices: 12.3 us -> 15.1 us  [exchange(): return lax.all_to_all(chunks, axes, 0, 0, tiled=True)]
  transfers between devices with their start and end apart: 1 -> 2, of which waited for: 1 -> 2; matrix products, arithmetic and copies ran while one was open for 0% -> 1% of each run, Pallas kernels for 0% -> 1%
where the time goes in v3:
time: 133 us
  blocking collectives  86.5 us (65%)
  starting transfers between devices  17.7 us (13%)
  waiting for transfers between devices  15.1 us (11%)
  Pallas kernels  10.6 us (8%)
  local copies, waits for them, and re-layouts  2.27 us (2%)
    all_to_all x3, blocking collectives, exchange(): return lax.all_to_all(chunks, axes, 0, 0, tiled=True)  44.4 us
    psum x1, blocking collectives, on_device(): far = lax.psum(near, FAR)  42.1 us
    all_to_all x2, starting transfers between devices, exchange(): return lax.all_to_all(chunks, axes, 0, 0, tiled=True)  17.7 us
    all_to_all x2, waiting for transfers between devices, exchange(): return lax.all_to_all(chunks, axes, 0, 0, tiled=True)  15.1 us
    pallas_call x7, Pallas kernels, call(): pl.pallas_call(kernel, out_shape=[jax.ShapeDtypeStruct(s, d) if i in far_...  10.6 us
  transfers between devices with their start and end apart: 2, of which 2 were waited for; matrix products, arithmetic and copies ran while one was open for 1% of the time, Pallas kernels for 1%

profile of v3, /device:TPU:1, one launch (start us, length us, event | category | flops | bytes accessed | tf_op | source)
XLA Modules:
  0.0 132.9 jit_solution(639077805231695193)
XLA Ops:
  0.6 0.0 copy-start
  0.6 0.9 copy-done
  1.5 2.5 %left_part.1 = (f32[32,8,128]{2,1,0:T(8,128)S(1)}, f32[512,512]{1,0:T(8,128)S(1)}) custom-call(f32[512,512]{1,0:T(8,128)} %momentum.1, bf16[512,512]{1,0:T(8,128)(2,1)} %gradient.1, f32[64,512]{1,0:T(8,128)S(1)} %bitcast.7), custom_call_target="tpu_custom_call" | custom-call | tf_op jit(solution)/shard_map/left_part/pallas_call | solution.py:48
  4.0 24.5 %all_to_all.25.parts = f32[32,8,128]{2,1,0:T(8,128)S(1)} all-to-all(f32[32,8,128]{2,1,0:T(8,128)S(1)} %get-tuple-element.15), channel_id=1, replica_groups=mesh['far'=8,'near'=4,'x'=4,'y'=4,'core'=2] {'x','y','core'}, dimensions={0} | all-to-all | bytes 262144 | tf_op jit(solution)/shard_map/all_to_all | solution.py:246
  28.6 11.2 %all_to_all.26.tiles = f32[32,8,128]{2,1,0:T(8,128)S(1)} all-to-all(f32[32,8,128]{2,1,0:T(8,128)S(1)} %left_tile.1), channel_id=1, replica_groups=mesh['far'=8,'near'=4,'x'=4,'y'=4,'core'=2] {'x','y','core'}, dimensions={0} | all-to-all | bytes 262144 | tf_op jit(solution)/shard_map/all_to_all | solution.py:246
  39.8 0.8 right_part.1
  40.7 8.6 %all_to_all.27 = f32[4,96,128]{2,1,0:T(8,128)S(1)} all-to-all(f32[4,96,128]{2,1,0:T(8,128)S(1)} %right_part.1), channel_id=1, replica_groups=mesh['far'=8,'near'=4,'x'=4,'y'=4,'core'=2] {'near'}, dimensions={0} | all-to-all | bytes 393216 | tf_op jit(solution)/shard_map/all_to_all | solution.py:246
  49.3 42.1 %psum.7 = f32[96,128]{1,0:T(8,128)S(1)} all-reduce(f32[96,128]{1,0:T(8,128)S(1)} %reduce_sum.9), channel_id=1, replica_groups=mesh['far'=8,'near'=4,'x'=4,'y'=4,'core'=2] {'far'}, use_global_device_ids=true, to_apply=%region_1.0 | all-reduce | flops 12288 | bytes 98304 | tf_op jit(solution)/shard_map/psum | solution.py:268
  91.4 0.7 broadcast_in_dim.2
  92.1 0.0 copy-start.1
  92.1 4.5 %all-to-all-start.3 = ((f32[4,64,128]{2,1,0:T(8,128)}), f32[4,64,128]{2,1,0:T(8,128)S(1)}, u32[]{:S(2)}, u32[]{:S(2)}) async-start(f32[4,64,128]{2,1,0:T(8,128)} %broadcast_in_dim.2), calls=%async_computation.3 | async-start | bytes 262144 | tf_op jit(solution)/shard_map/all_to_all | solution.py:246
  96.6 1.7 %first_factor_of.1 = (f32[64,64]{1,0:T(8,128)S(1)}, f32[64,64]{1,0:T(8,128)S(1)}) custom-call(f32[32,128]{1,0:T(8,128)S(1)} %slice.9.gram), custom_call_target="tpu_custom_call" | custom-call | tf_op jit(solution)/shard_map/first_factor_of/pallas_call | solution.py:48
  98.3 3.0 %all-to-all-done.3 = f32[4,64,128]{2,1,0:T(8,128)S(1)} async-done(((f32[4,64,128]{2,1,0:T(8,128)}), f32[4,64,128]{2,1,0:T(8,128)S(1)}, u32[]{:S(2)}, u32[]{:S(2)}) %all-to-all-start.3) | async-done | bytes 131104 | tf_op jit(solution)/shard_map/all_to_all | solution.py:246
  101.4 0.0 copy-done.1
  101.4 1.6 %second_gram.1 = (f32[64,512]{1,0:T(8,128)S(1)}, f32[32,40,128]{2,1,0:T(8,128)}) custom-call(f32[32,8,128]{2,1,0:T(8,128)S(1)} %bitcast.6, f32[64,64]{1,0:T(8,128)S(1)} %get-tuple-element.17.inverse_one, f32[64,512]{1,0:T(8,128)S(1)} %bitcast.8), custom_call_target="tpu_custom_call" | custom-call | tf_op jit(solution)/shard_map/second_gram/pallas_call | solution.py:48
  103.0 13.2 %all-to-all-start.4 = ((f32[32,40,128]{2,1,0:T(8,128)}), f32[32,40,128]{2,1,0:T(8,128)S(1)}, u32[]{:S(2)}, u32[]{:S(2)}) async-start(f32[32,40,128]{2,1,0:T(8,128)} %get-tuple-element.18), calls=%async_computation.4 | async-start | bytes 1310720 | tf_op jit(solution)/shard_map/all_to_all | solution.py:246
  116.2 0.7 copy.8
  116.9 0.3 left_once.1.left_one
  117.2 12.1 %all-to-all-done.4.pairs = f32[32,40,128]{2,1,0:T(8,128)S(1)} async-done(((f32[32,40,128]{2,1,0:T(8,128)}), f32[32,40,128]{2,1,0:T(8,128)S(1)}, u32[]{:S(2)}, u32[]{:S(2)}) %all-to-all-start.4) | async-done | bytes 655392 | tf_op jit(solution)/shard_map/all_to_all | solution.py:246
  129.2 3.7 %results.1 = (bf16[512,512]{1,0:T(8,128)(2,1)}, f32[64,512]{1,0:T(8,128)}, f32[64,512]{1,0:T(8,128)}, f32[512,512]{1,0:T(8,128)}) custom-call(f32[32,40,128]{2,1,0:T(8,128)S(1)} %all-to-all-done.4.pairs, f32[64,512]{1,0:T(8,128)S(1)} %left_once.1.left_one, f32[64,512]{1,0:T(8,128)S(1)} %get-tuple-element.19.right_one, f32[512,512]{1,0:T(8,128)S(1)} %get-tuple-element.16.blended), custom_call_target="tpu_custom_call" | custom-call | tf_op jit(solution)/shard_map/results/pallas_call | solution.py:48
  (5 shorter events, 0.1 us)
Async XLA Ops:
  0.6 0.9 copy-start
  92.1 9.3 %copy-start.1 = (f32[512,64]{0,1:T(8,128)S(1)}, f32[512,64]{0,1:T(8,128)}, u32[]{:S(2)}) copy-start(f32[512,64]{0,1:T(8,128)} %param.5) | copy-start | bytes 393220
  92.1 9.3 %all-to-all-start.3 = ((f32[4,64,128]{2,1,0:T(8,128)}), f32[4,64,128]{2,1,0:T(8,128)S(1)}, u32[]{:S(2)}, u32[]{:S(2)}) async-start(f32[4,64,128]{2,1,0:T(8,128)} %broadcast_in_dim.2), calls=%async_computation.3 | async-start | bytes 262144 | tf_op jit(solution)/shard_map/all_to_all | solution.py:246
  103.0 26.2 %all-to-all-start.4 = ((f32[32,40,128]{2,1,0:T(8,128)}), f32[32,40,128]{2,1,0:T(8,128)S(1)}, u32[]{:S(2)}, u32[]{:S(2)}) async-start(f32[32,40,128]{2,1,0:T(8,128)} %get-tuple-element.18), calls=%async_computation.4 | async-start | bytes 1310720 | tf_op jit(solution)/shard_map/all_to_all | solution.py:246

commit v4 on v3

--- a/solution.py
+++ b/solution.py
@@ -148,10 +148,58 @@
         copies[i] = tile
 
 
+def slices(a, axis, lead):
+    bound = jnp.max(jnp.abs(a), axis=axis, keepdims=True)
+    shift = bound * 2.0**lead
+    parts = []
+    for _ in range(4):
+        part = (a + shift) - shift
+        parts.append(part.astype(jnp.bfloat16))
+        a = a - part
+        shift = shift * 2.0 ** (lead - 25)
+    return parts
+
+
+def two_sum(a, b):
+    total = a + b
+    back = total - a
+    return total, (a - (total - back)) + (b - back)
+
+
+def total_of(terms):
+    high, low = None, None
+    for term in terms:
+        a, b = term if isinstance(term, tuple) else (term, None)
+        if high is None:
+            high, low = a, (jnp.zeros_like(a) if b is None else b)
+            continue
+        high, error = two_sum(high, a)
+        low = low + (error if b is None else error + b)
+    top = high + low
+    return top, low - (top - high)
+
+
+def block_sum(blocks):
+    wide = [
+        total_of([blocks[64 * i : 64 * i + 64, 128 * j : 128 * j + 128] for i in range(4)])
+        for j in range(2)
+    ]
+    high, low = total_of(wide)
+    return total_of([(high[:, :64], low[:, :64]), (high[:, 64:], low[:, 64:])])
+
+
+def exact(a, b, dims):
+    return block_sum(
+        lax.dot_general(a, b, (dims, ((), ())), preferred_element_type=F32)
+    )
+
+
 def right_part(tiles, blended, send):
     left_raw = read_tiles(tiles)
     product = nn(left_raw, blended[...])
-    gram = fold(nt(left_raw, left_raw))
+    parts = jnp.concatenate(slices(left_raw, 1, 18), axis=0)
+    high, low = exact(parts, parts, ((1,), (1,)))
+    gram = jnp.concatenate([fold(high), fold(low)], axis=0)
     for i in range(8):
         for j in range(4):
             tile = product[8 * i : 8 * i + 8, 128 * j : 128 * j + 128]
@@ -160,30 +208,54 @@
         send[i, 64:] = gram
 
 
-def first_factor_of(gram, upper_one, inverse_one):
-    upper, inverse = factor(unfold(gram[...]))
+def sum_of(chunks, n, total):
+    high, low = total_of([(chunks[i, 64:96], chunks[i, 96:128]) for i in range(n)])
+    value = chunks[0, :64]
+    for i in range(1, n):
+        value = value + chunks[i, :64]
+    total[:64] = value
+    total[64:96] = high
+    total[96:128] = low
+
+
+def near_sum(chunks, total):
+    sum_of(chunks, 4, total)
+
+
+def far_sum(chunks, copies, gram):
+    high, low = total_of([(chunks[i, 64:96], chunks[i, 96:128]) for i in range(8)])
+    gram[:32] = high
+    gram[32:] = low
+    value = chunks[0, :64]
+    for i in range(1, 8):
+        value = value + chunks[i, :64]
+    for i in range(4):
+        copies[i] = value
+
+
+def factors(gram, upper_one, inverse_one, inverse_two):
+    high, low = unfold(gram[:32]), unfold(gram[32:])
+    upper, inverse = factor(high)
     upper_one[...] = upper
     inverse_one[...] = inverse
-
-
-def second_gram(total, inverse_one, factor_t, right_one, copies):
-    inverse = inverse_one[...]
-    right = nn(inverse, read_tiles(total))
-    right_one[...] = right
-    gram_two = nt(nn(inverse, factor_t[...]), right)
-    squared = nt(right, right)
-    row, lane = places((RANK, RANK))
-    diagonal = jnp.sum(jnp.where(row == lane, squared, 0.0), axis=0, keepdims=True)
-    pair = fold(jnp.where(row <= lane, gram_two, squared))
-    last = jnp.concatenate([diagonal, jnp.zeros((1, 64), F32)], axis=1)
-    last = jnp.broadcast_to(last, (8, 128))
+    columns = jnp.concatenate(slices(upper, 0, 17), axis=1)
+    square_high, square_low = exact(columns, columns, ((0,), (0,)))
+    rest, error = two_sum(high, -square_high)
+    rest = rest + (error + (low - square_low))
+    lines = jnp.concatenate(slices(upper, 1, 17), axis=0)
+    unit, _ = exact(jnp.concatenate(slices(inverse, 1, 17), axis=0), lines, ((1,), (1,)))
+    gram_two = nt(unit, unit) + nt(nn(inverse, rest), inverse)
+    _, second = factor(gram_two)
+    inverse_two[...] = second
+
+
+def right_of(total, inverse_one, inverse_two, right, copies):
+    right_t = nn(inverse_two[...], nn(inverse_one[...], read_tiles(total)))
+    right[...] = right_t
+    squares = nt(jnp.ones((8, SIDE), F32), right_t * right_t)
+    squares = jnp.concatenate([squares, jnp.zeros((8, 64), F32)], axis=1)
     for i in range(32):
-        copies[i, :32] = pair
-        copies[i, 32:] = last
-
-
-def left_once(tiles, inverse_one, left_one):
-    left_one[...] = nn(inverse_one[...], read_tiles(tiles))
+        copies[i] = squares
 
 
 def halves(a):
@@ -191,53 +263,49 @@
     return high, (a - high.astype(F32)).astype(jnp.bfloat16)
 
 
-def results(
-    pairs, left_one, right_one, blended,
-    update, left, normed, new_momentum, u, l, n, m, sems,
-):
-    pair = jnp.sum(pairs[...], axis=0)
-    mixed = unfold(pair[:32])
-    diagonal = pair[32:33, :64]
+def products(left_t, other, i):
+    high, low = halves(left_t[:, STEP * i : STEP * i + STEP])
+    lefts = jnp.concatenate([high, high, low], axis=0)
+    high, low = halves(other)
+    others = jnp.concatenate([high, low, high], axis=0)
+    return lax.dot_general(
+        lefts, others, (((0,), (0,)), ((), ())), preferred_element_type=F32
+    )
+
+
+def write_back(pairs, sems):
+    copies = [pltpu.make_async_copy(a, b, sems.at[k]) for k, (a, b) in enumerate(pairs)]
+    for copy in copies:
+        copy.start()
+    return copies
+
+
+def momentum_of(tiles, inverse_one, inverse_two, right, blended, left, out, new_momentum, m, sems):
+    left_t = nn(inverse_two[...], nn(inverse_one[...], read_tiles(tiles)))
+    left[...] = left_t
+    copies = write_back([(left, out)], sems.at[STEPS])
+    scaled = 0.05 * right[...]
+    for i in range(STEPS):
+        m[rows_of(i)] = blended[rows_of(i)] - products(left_t, scaled, i)
+        copies += write_back([(m.at[rows_of(i)], new_momentum.at[rows_of(i)])], sems.at[i])
+    for copy in copies:
+        copy.wait()
+
+
+def update_of(parts, left, right, update, normed, u, n, sems):
+    squares = parts[0, :1]
+    for i in range(1, 32):
+        squares = squares + parts[i, :1]
     row, lane = places((RANK, RANK))
-    flipped = mixed.T
-    gram_two = jnp.where(row <= lane, mixed, flipped)
-    squared = jnp.where(row > lane, mixed, flipped)
-    squared = jnp.where(row == lane, diagonal, squared)
-    _, inverse = factor(gram_two)
-    squares = jnp.sum(nn(inverse, squared) * inverse, axis=1, keepdims=True)
-    left_t = nn(inverse, left_one[...])
-    right_t = nn(inverse, right_one[...])
-    normed_t = right_t / (jnp.sqrt(squares) + 1e-06)
-    l[...] = left_t
+    squares = jnp.sum(jnp.where(row == lane, squares[:, :64], 0.0), axis=1, keepdims=True)
+    normed_t = right[...] / (jnp.sqrt(squares) + 1e-06)
     n[...] = normed_t
-    copies = [
-        pltpu.make_async_copy(l, left, sems.at[0, 0]),
-        pltpu.make_async_copy(n, normed, sems.at[0, 1]),
-    ]
-    for copy in copies:
-        copy.start()
-    high, low = halves(left_t)
-    lefts = jnp.concatenate([high, high, low], axis=0)
-    high, low = halves(0.05 * right_t)
-    rights = jnp.concatenate([high, low, high], axis=0)
-    high, low = halves(math.sqrt(NROW * NCOL / RANK) * normed_t)
-    norms = jnp.concatenate([high, low, high], axis=0)
-
-    def product(i, other):
-        part = lefts[:, STEP * i : STEP * i + STEP]
-        return lax.dot_general(
-            part, other, (((0,), (0,)), ((), ())), preferred_element_type=F32
-        )
-
+    copies = write_back([(n, normed)], sems.at[STEPS])
+    scaled = math.sqrt(NROW * NCOL / RANK) * normed_t
+    left_t = left[...]
     for i in range(STEPS):
-        m[rows_of(i)] = blended[rows_of(i)] - product(i, rights)
-        u[rows_of(i)] = product(i, norms).astype(jnp.bfloat16)
-        for k, (source, target) in enumerate(((m, new_momentum), (u, update))):
-            copy = pltpu.make_async_copy(
-                source.at[rows_of(i)], target.at[rows_of(i)], sems.at[1 + i, k]
-            )
-            copy.start()
-            copies.append(copy)
+        u[rows_of(i)] = products(left_t, scaled, i).astype(jnp.bfloat16)
+        copies += write_back([(u.at[rows_of(i)], update.at[rows_of(i)])], sems.at[i])
     for copy in copies:
         copy.wait()
 
@@ -263,31 +331,35 @@
     )
     (copies,) = call(left_tile, [tiled], exchange(part, COL))
     tiles = exchange(copies, COL)
-    (send,) = call(right_part, [((4, 96, 128), F32)], tiles, blended)
-    near = jnp.sum(exchange(send, NEAR), axis=0)
-    far = lax.psum(near, FAR)
-    quarters = jnp.broadcast_to(far[None, :64], (4, 64, 128))
+    chunk = (128, 128)
+    (send,) = call(right_part, [((4,) + chunk, F32)], tiles, blended)
+    (near,) = call(near_sum, [(chunk, F32)], exchange(send, NEAR))
+    quarters, gram = call(
+        far_sum, [((4, 64, 128), F32), ((64, 128), F32)], lax.all_gather(near, FAR)
+    )
     total = exchange(quarters, NEAR).reshape(32, 8, 128)
-    upper_one, inverse_one = call(
-        first_factor_of, [(square, F32), (square, F32)], far[64:]
-    )
+    upper_one, inverse_one, inverse_two = call(factors, [(square, F32)] * 3, gram)
     first_factor = upper_one.T / jnp.sqrt(F32(NROW) * F32(NCOL))
-    right_one, copies = call(
-        second_gram, [(flat, F32), ((32, 40, 128), F32)], total, inverse_one, factor_t
-    )
-    pairs = exchange(copies, COL)
-    (left_one,) = call(left_once, [(flat, F32)], tiles, inverse_one)
-    update, left_t, normed_t, new_momentum = call(
-        results,
-        [(full, jnp.bfloat16), (flat, F32), (flat, F32), (full, F32)],
-        pairs, left_one, right_one, blended,
-        far_out=(0, 1, 2, 3),
+    right_t, copies = call(
+        right_of, [(flat, F32), tiled], total, inverse_one, inverse_two
+    )
+    parts = exchange(copies, COL)
+    left_in, left_t, new_momentum = call(
+        momentum_of,
+        [(flat, F32), (flat, F32), (full, F32)],
+        tiles, inverse_one, inverse_two, right_t, blended,
+        far_out=(1, 2),
+        scratch=[pltpu.VMEM(full, F32), pltpu.SemaphoreType.DMA((STEPS + 1, 1))],
+    )
+    update, normed_t = call(
+        update_of,
+        [(full, jnp.bfloat16), (flat, F32)],
+        parts, left_in, right_t,
+        far_out=(0, 1),
         scratch=[
             pltpu.VMEM(full, jnp.bfloat16),
             pltpu.VMEM(flat, F32),
-            pltpu.VMEM(flat, F32),
-            pltpu.VMEM(full, F32),
-            pltpu.SemaphoreType.DMA((1 + STEPS, 2)),
+            pltpu.SemaphoreType.DMA((STEPS + 1, 1)),
         ],
     )
     return (update, left_t.T, normed_t.T, new_momentum, first_factor)

time: 133 us -> 127 us (0.955)
  waiting for transfers between devices: 15.1 us -> 5.61 us
  blocking collectives: 86.5 us -> 90.9 us
  starting transfers between devices: 17.7 us -> 14.6 us
  Pallas kernels: 10.6 us -> 13.2 us
    all_gather x0 -> x1, blocking collectives: none -> 45.4 us  [on_device(): lax.all_gather(near, FAR)]
    psum x1 -> x0, blocking collectives: 42.1 us -> none  [on_device(): far = lax.psum(near, FAR)]
    all_to_all x2, waiting for transfers between devices: 15.1 us -> 5.61 us  [exchange(): return lax.all_to_all(chunks, axes, 0, 0, tiled=True)]
    all_to_all x2, starting transfers between devices: 17.7 us -> 14.6 us  [exchange(): return lax.all_to_all(chunks, axes, 0, 0, tiled=True)]
    pallas_call x7 -> x9, Pallas kernels: 10.6 us -> 13.2 us  [call(): pl.pallas_call(kernel, out_shape=[jax.ShapeDtypeStruct(s, d) if i in far_...]
  transfers between devices with their start and end apart: 2 -> 2, of which waited for: 2 -> 2; matrix products, arithmetic and copies ran while one was open for 1% -> 1% of each run, Pallas kernels for 1% -> 5%
where the time goes in v4:
time: 127 us
  blocking collectives  90.9 us (72%)
  starting transfers between devices  14.6 us (11%)
  Pallas kernels  13.2 us (10%)
  waiting for transfers between devices  5.61 us (4%)
  local copies, waits for them, and re-layouts  1.6 us (1%)
    all_to_all x3, blocking collectives, exchange(): return lax.all_to_all(chunks, axes, 0, 0, tiled=True)  45.5 us
    all_gather x1, blocking collectives, on_device(): lax.all_gather(near, FAR)  45.4 us
    all_to_all x2, starting transfers between devices, exchange(): return lax.all_to_all(chunks, axes, 0, 0, tiled=True)  14.6 us
    pallas_call x9, Pallas kernels, call(): pl.pallas_call(kernel, out_shape=[jax.ShapeDtypeStruct(s, d) if i in far_...  13.2 us
    all_to_all x2, waiting for transfers between devices, exchange(): return lax.all_to_all(chunks, axes, 0, 0, tiled=True)  5.61 us
  transfers between devices with their start and end apart: 2, of which 2 were waited for; matrix products, arithmetic and copies ran while one was open for 1% of the time, Pallas kernels for 5%

profile of v4, /device:TPU:1, one launch (start us, length us, event | category | flops | bytes accessed | tf_op | source)
XLA Modules:
  0.0 126.6 jit_solution(1167149176921943902)
XLA Ops:
  0.6 0.0 copy-start
  0.6 0.9 copy-done
  1.5 2.5 %left_part.1 = (f32[32,8,128]{2,1,0:T(8,128)S(1)}, f32[512,512]{1,0:T(8,128)S(1)}) custom-call(f32[512,512]{1,0:T(8,128)} %momentum.1, bf16[512,512]{1,0:T(8,128)(2,1)} %gradient.1, f32[64,512]{1,0:T(8,128)S(1)} %bitcast.9), custom_call_target="tpu_custom_call" | custom-call | tf_op jit(solution)/shard_map/left_part/pallas_call | solution.py:48
  4.0 24.5 %all_to_all.25.parts = f32[32,8,128]{2,1,0:T(8,128)S(1)} all-to-all(f32[32,8,128]{2,1,0:T(8,128)S(1)} %get-tuple-element.19), channel_id=1, replica_groups=mesh['far'=8,'near'=4,'x'=4,'y'=4,'core'=2] {'x','y','core'}, dimensions={0} | all-to-all | bytes 262144 | tf_op jit(solution)/shard_map/all_to_all | solution.py:314
  28.6 11.2 %all_to_all.26.tiles = f32[32,8,128]{2,1,0:T(8,128)S(1)} all-to-all(f32[32,8,128]{2,1,0:T(8,128)S(1)} %left_tile.1), channel_id=1, replica_groups=mesh['far'=8,'near'=4,'x'=4,'y'=4,'core'=2] {'x','y','core'}, dimensions={0} | all-to-all | bytes 262144 | tf_op jit(solution)/shard_map/all_to_all | solution.py:314
  39.8 1.2 right_part.1
  41.0 9.8 %all_to_all.27.chunks = f32[4,128,128]{2,1,0:T(8,128)S(1)} all-to-all(f32[4,128,128]{2,1,0:T(8,128)S(1)} %right_part.1), channel_id=1, replica_groups=mesh['far'=8,'near'=4,'x'=4,'y'=4,'core'=2] {'near'}, dimensions={0} | all-to-all | bytes 524288 | tf_op jit(solution)/shard_map/all_to_all | solution.py:314
  50.8 45.4 %all-gather = f32[1024,128]{1,0:T(8,128)S(1)} all-gather(f32[128,128]{1,0:T(8,128)S(1)} %near_sum.1), channel_id=2, replica_groups=mesh['far'=8,'near'=4,'x'=4,'y'=4,'core'=2] {'far'}, dimensions={0}, use_global_device_ids=true | all-gather | bytes 589824 | tf_op jit(solution)/shard_map/all_gather | solution.py:338
  96.2 0.7 far_sum.1
  96.9 3.3 %all-to-all-start.3 = ((f32[4,64,128]{2,1,0:T(8,128)}), f32[4,64,128]{2,1,0:T(8,128)S(1)}, u32[]{:S(2)}, u32[]{:S(2)}) async-start(f32[4,64,128]{2,1,0:T(8,128)} %get-tuple-element.21), calls=%async_computation.3 | async-start | bytes 262144 | tf_op jit(solution)/shard_map/all_to_all | solution.py:314
  100.2 4.5 %factors.1 = (f32[64,64]{1,0:T(8,128)S(1)}, f32[64,64]{1,0:T(8,128)S(1)}, f32[64,64]{1,0:T(8,128)S(1)}) custom-call(f32[64,128]{1,0:T(8,128)S(1)} %get-tuple-element.22.gram), custom_call_target="tpu_custom_call" | custom-call | tf_op jit(solution)/shard_map/factors/pallas_call | solution.py:48
  104.7 0.3 all-to-all-done.3
  104.9 1.4 %right_of.1 = (f32[64,512]{1,0:T(8,128)S(1)}, f32[32,8,128]{2,1,0:T(8,128)}) custom-call(f32[32,8,128]{2,1,0:T(8,128)S(1)} %bitcast.8, f32[64,64]{1,0:T(8,128)S(1)} %get-tuple-element.23.inverse_one, f32[64,64]{1,0:T(8,128)S(1)} %get-tuple-element.24.inverse_two), custom_call_target="tpu_custom_call" | custom-call | tf_op jit(solution)/shard_map/right_of/pallas_call | solution.py:48
  106.3 11.3 %all-to-all-start.4 = ((f32[32,8,128]{2,1,0:T(8,128)}), f32[32,8,128]{2,1,0:T(8,128)S(1)}, u32[]{:S(2)}, u32[]{:S(2)}) async-start(f32[32,8,128]{2,1,0:T(8,128)} %get-tuple-element.25), calls=%async_computation.4 | async-start | bytes 262144 | tf_op jit(solution)/shard_map/all_to_all | solution.py:314
  117.7 0.7 copy.8
  118.4 1.7 %momentum_of.1 = (f32[64,512]{1,0:T(8,128)S(1)}, f32[64,512]{1,0:T(8,128)}, f32[512,512]{1,0:T(8,128)}) custom-call(f32[32,8,128]{2,1,0:T(8,128)S(1)} %all_to_all.26.tiles, f32[64,64]{1,0:T(8,128)S(1)} %get-tuple-element.23.inverse_one, f32[64,64]{1,0:T(8,128)S(1)} %get-tuple-element.24.inverse_two, f32[64,512]{1,0:T(8,128)S(1)} %get-tuple-element.26.right, ...), custom_call_target="tpu_custom_call" | custom-call | tf_op jit(solution)/shard_map/momentum_of/pallas_call | solution.py:48
  120.1 5.3 %all-to-all-done.4.parts = f32[32,8,128]{2,1,0:T(8,128)S(1)} async-done(((f32[32,8,128]{2,1,0:T(8,128)}), f32[32,8,128]{2,1,0:T(8,128)S(1)}, u32[]{:S(2)}, u32[]{:S(2)}) %all-to-all-start.4) | async-done | bytes 131104 | tf_op jit(solution)/shard_map/all_to_all | solution.py:314
  125.5 1.2 update_of.1
  (3 shorter events, 0.1 us)
Async XLA Ops:
  0.6 0.9 copy-start
  96.9 8.1 %all-to-all-start.3 = ((f32[4,64,128]{2,1,0:T(8,128)}), f32[4,64,128]{2,1,0:T(8,128)S(1)}, u32[]{:S(2)}, u32[]{:S(2)}) async-start(f32[4,64,128]{2,1,0:T(8,128)} %get-tuple-element.21), calls=%async_computation.3 | async-start | bytes 262144 | tf_op jit(solution)/shard_map/all_to_all | solution.py:314
  106.3 19.1 %all-to-all-start.4 = ((f32[32,8,128]{2,1,0:T(8,128)}), f32[32,8,128]{2,1,0:T(8,128)S(1)}, u32[]{:S(2)}, u32[]{:S(2)}) async-start(f32[32,8,128]{2,1,0:T(8,128)} %get-tuple-element.25), calls=%async_computation.4 | async-start | bytes 262144 | tf_op jit(solution)/shard_map/all_to_all | solution.py:314

commit v5 on v4

--- a/solution.py
+++ b/solution.py
@@ -128,18 +128,20 @@
     return pl.ds(STEP * i, STEP)
 
 
-def left_part(momentum, gradient, factor_t, part, blended, old, change, sems):
-    copies = [
-        pltpu.make_async_copy(momentum, old, sems.at[0]),
-        pltpu.make_async_copy(gradient, change, sems.at[1]),
-    ]
+def start_copies(pairs, sems):
+    copies = [pltpu.make_async_copy(a, b, sems.at[k]) for k, (a, b) in enumerate(pairs)]
     for copy in copies:
         copy.start()
-    for copy in copies:
+    return copies
+
+
+def left_part(momentum, gradient, factor_t, part, blended, old, change, right, sems):
+    pairs = ((momentum, old), (gradient, change), (factor_t, right))
+    for copy in start_copies(pairs, sems):
         copy.wait()
     block = old[...] + change[...].astype(F32)
     blended[...] = block
-    write_tiles(part, nt(factor_t[...], block))
+    write_tiles(part, nt(right[...], block))
 
 
 def left_tile(parts, copies):
@@ -254,8 +256,8 @@
     right[...] = right_t
     squares = nt(jnp.ones((8, SIDE), F32), right_t * right_t)
     squares = jnp.concatenate([squares, jnp.zeros((8, 64), F32)], axis=1)
-    for i in range(32):
-        copies[i] = squares
+    for i in range(4):
+        copies[8 * i : 8 * i + 8] = squares
 
 
 def halves(a):
@@ -273,39 +275,30 @@
     )
 
 
-def write_back(pairs, sems):
-    copies = [pltpu.make_async_copy(a, b, sems.at[k]) for k, (a, b) in enumerate(pairs)]
-    for copy in copies:
-        copy.start()
-    return copies
-
-
 def momentum_of(tiles, inverse_one, inverse_two, right, blended, left, out, new_momentum, m, sems):
     left_t = nn(inverse_two[...], nn(inverse_one[...], read_tiles(tiles)))
     left[...] = left_t
-    copies = write_back([(left, out)], sems.at[STEPS])
+    copies = start_copies([(left, out)], sems.at[STEPS])
     scaled = 0.05 * right[...]
     for i in range(STEPS):
         m[rows_of(i)] = blended[rows_of(i)] - products(left_t, scaled, i)
-        copies += write_back([(m.at[rows_of(i)], new_momentum.at[rows_of(i)])], sems.at[i])
+        copies += start_copies([(m.at[rows_of(i)], new_momentum.at[rows_of(i)])], sems.at[i])
     for copy in copies:
         copy.wait()
 
 
 def update_of(parts, left, right, update, normed, u, n, sems):
-    squares = parts[0, :1]
-    for i in range(1, 32):
-        squares = squares + parts[i, :1]
+    squares = jnp.sum(parts[...], axis=0, keepdims=True)
     row, lane = places((RANK, RANK))
     squares = jnp.sum(jnp.where(row == lane, squares[:, :64], 0.0), axis=1, keepdims=True)
     normed_t = right[...] / (jnp.sqrt(squares) + 1e-06)
     n[...] = normed_t
-    copies = write_back([(n, normed)], sems.at[STEPS])
+    copies = start_copies([(n, normed)], sems.at[STEPS])
     scaled = math.sqrt(NROW * NCOL / RANK) * normed_t
     left_t = left[...]
     for i in range(STEPS):
         u[rows_of(i)] = products(left_t, scaled, i).astype(jnp.bfloat16)
-        copies += write_back([(u.at[rows_of(i)], update.at[rows_of(i)])], sems.at[i])
+        copies += start_copies([(u.at[rows_of(i)], update.at[rows_of(i)])], sems.at[i])
     for copy in copies:
         copy.wait()
 
@@ -322,11 +315,12 @@
         left_part,
         [tiled, (full, F32)],
         momentum, gradient, factor_t,
-        far_in=(0, 1),
+        far_in=(0, 1, 2),
         scratch=[
             pltpu.VMEM(full, F32),
             pltpu.VMEM(full, jnp.bfloat16),
-            pltpu.SemaphoreType.DMA((2,)),
+            pltpu.VMEM(flat, F32),
+            pltpu.SemaphoreType.DMA((3,)),
         ],
     )
     (copies,) = call(left_tile, [tiled], exchange(part, COL))
@@ -341,9 +335,9 @@
     upper_one, inverse_one, inverse_two = call(factors, [(square, F32)] * 3, gram)
     first_factor = upper_one.T / jnp.sqrt(F32(NROW) * F32(NCOL))
     right_t, copies = call(
-        right_of, [(flat, F32), tiled], total, inverse_one, inverse_two
-    )
-    parts = exchange(copies, COL)
+        right_of, [(flat, F32), ((32, 128), F32)], total, inverse_one, inverse_two
+    )
+    parts = exchange(copies.reshape(32, 1, 128), COL).reshape(32, 128)
     left_in, left_t, new_momentum = call(
         momentum_of,
         [(flat, F32), (flat, F32), (full, F32)],

time: 127 us -> 125 us (0.984)
  no operation moved by 1% of the time
where the time goes in v5:
time: 125 us
  blocking collectives  90.7 us (73%)
  starting transfers between devices  14.8 us (12%)
  Pallas kernels  13.1 us (10%)
  waiting for transfers between devices  4.84 us (4%)
    all_to_all x3, blocking collectives, exchange(): return lax.all_to_all(chunks, axes, 0, 0, tiled=True)  45.5 us
    all_gather x1, blocking collectives, on_device(): lax.all_gather(near, FAR)  45.1 us
    all_to_all x2, starting transfers between devices, exchange(): return lax.all_to_all(chunks, axes, 0, 0, tiled=True)  14.8 us
    pallas_call x9, Pallas kernels, call(): pl.pallas_call(kernel, out_shape=[jax.ShapeDtypeStruct(s, d) if i in far_...  13.1 us
    all_to_all x2, waiting for transfers between devices, exchange(): return lax.all_to_all(chunks, axes, 0, 0, tiled=True)  4.84 us
  transfers between devices with their start and end apart: 2, of which 2 were waited for; matrix products, arithmetic and copies ran while one was open for 1% of the time, Pallas kernels for 5%

profile of v5, /device:TPU:1, one launch (start us, length us, event | category | flops | bytes accessed | tf_op | source)
XLA Modules:
  0.0 124.8 jit_solution(8253397165545685150)
XLA Ops:
  0.6 2.5 %left_part.1 = (f32[32,8,128]{2,1,0:T(8,128)S(1)}, f32[512,512]{1,0:T(8,128)S(1)}) custom-call(f32[512,512]{1,0:T(8,128)} %momentum.1, bf16[512,512]{1,0:T(8,128)(2,1)} %gradient.1, f32[64,512]{1,0:T(8,128)} %bitcast.14), custom_call_target="tpu_custom_call" | custom-call | tf_op jit(solution)/shard_map/left_part/pallas_call | solution.py:48
  3.1 24.5 %all_to_all.25.parts = f32[32,8,128]{2,1,0:T(8,128)S(1)} all-to-all(f32[32,8,128]{2,1,0:T(8,128)S(1)} %get-tuple-element.19), channel_id=1, replica_groups=mesh['far'=8,'near'=4,'x'=4,'y'=4,'core'=2] {'x','y','core'}, dimensions={0} | all-to-all | bytes 262144 | tf_op jit(solution)/shard_map/all_to_all | solution.py:307
  27.7 11.2 %all_to_all.26.tiles = f32[32,8,128]{2,1,0:T(8,128)S(1)} all-to-all(f32[32,8,128]{2,1,0:T(8,128)S(1)} %left_tile.1), channel_id=1, replica_groups=mesh['far'=8,'near'=4,'x'=4,'y'=4,'core'=2] {'x','y','core'}, dimensions={0} | all-to-all | bytes 262144 | tf_op jit(solution)/shard_map/all_to_all | solution.py:307
  39.0 1.2 right_part.1
  40.1 9.8 %all_to_all.27.chunks = f32[4,128,128]{2,1,0:T(8,128)S(1)} all-to-all(f32[4,128,128]{2,1,0:T(8,128)S(1)} %right_part.1), channel_id=1, replica_groups=mesh['far'=8,'near'=4,'x'=4,'y'=4,'core'=2] {'near'}, dimensions={0} | all-to-all | bytes 524288 | tf_op jit(solution)/shard_map/all_to_all | solution.py:307
  49.9 45.1 %all-gather = f32[1024,128]{1,0:T(8,128)S(1)} all-gather(f32[128,128]{1,0:T(8,128)S(1)} %near_sum.1), channel_id=2, replica_groups=mesh['far'=8,'near'=4,'x'=4,'y'=4,'core'=2] {'far'}, dimensions={0}, use_global_device_ids=true | all-gather | bytes 589824 | tf_op jit(solution)/shard_map/all_gather | solution.py:332
  95.1 0.7 far_sum.1
  95.8 3.3 %all-to-all-start.3 = ((f32[4,64,128]{2,1,0:T(8,128)}), f32[4,64,128]{2,1,0:T(8,128)S(1)}, u32[]{:S(2)}, u32[]{:S(2)}) async-start(f32[4,64,128]{2,1,0:T(8,128)} %get-tuple-element.21), calls=%async_computation.3 | async-start | bytes 262144 | tf_op jit(solution)/shard_map/all_to_all | solution.py:307
  99.1 4.5 %factors.1 = (f32[64,64]{1,0:T(8,128)S(1)}, f32[64,64]{1,0:T(8,128)S(1)}, f32[64,64]{1,0:T(8,128)S(1)}) custom-call(f32[64,128]{1,0:T(8,128)S(1)} %get-tuple-element.22.gram), custom_call_target="tpu_custom_call" | custom-call | tf_op jit(solution)/shard_map/factors/pallas_call | solution.py:48
  103.5 0.3 all-to-all-done.3
  103.8 1.3 %right_of.1 = (f32[64,512]{1,0:T(8,128)S(1)}, f32[32,128]{1,0:T(8,128)}) custom-call(f32[32,8,128]{2,1,0:T(8,128)S(1)} %bitcast.12, f32[64,64]{1,0:T(8,128)S(1)} %get-tuple-element.23.inverse_one, f32[64,64]{1,0:T(8,128)S(1)} %get-tuple-element.24.inverse_two), custom_call_target="tpu_custom_call" | custom-call | tf_op jit(solution)/shard_map/right_of/pallas_call | solution.py:48
  105.2 11.5 %all-to-all-start.4 = ((f32[32,1,128]{2,1,0:T(1,128)}), f32[32,1,128]{2,1,0:T(1,128)S(1)}, u32[]{:S(2)}, u32[]{:S(2)}) async-start(f32[32,1,128]{2,1,0:T(1,128)} %bitcast.4), calls=%async_computation.4 | async-start | bytes 32768 | tf_op jit(solution)/shard_map/all_to_all | solution.py:307
  116.7 0.7 copy.10
  117.4 1.7 %momentum_of.1 = (f32[64,512]{1,0:T(8,128)S(1)}, f32[64,512]{1,0:T(8,128)}, f32[512,512]{1,0:T(8,128)}) custom-call(f32[32,8,128]{2,1,0:T(8,128)S(1)} %all_to_all.26.tiles, f32[64,64]{1,0:T(8,128)S(1)} %get-tuple-element.23.inverse_one, f32[64,64]{1,0:T(8,128)S(1)} %get-tuple-element.24.inverse_two, f32[64,512]{1,0:T(8,128)S(1)} %get-tuple-element.26.right, ...), custom_call_target="tpu_custom_call" | custom-call | tf_op jit(solution)/shard_map/momentum_of/pallas_call | solution.py:48
  119.1 4.6 %all-to-all-done.4 = f32[32,1,128]{2,1,0:T(1,128)S(1)} async-done(((f32[32,1,128]{2,1,0:T(1,128)}), f32[32,1,128]{2,1,0:T(1,128)S(1)}, u32[]{:S(2)}, u32[]{:S(2)}) %all-to-all-start.4) | async-done | bytes 16416 | tf_op jit(solution)/shard_map/all_to_all | solution.py:307
  123.7 1.1 update_of.1
  (3 shorter events, 0.1 us)
Async XLA Ops:
  95.8 8.1 %all-to-all-start.3 = ((f32[4,64,128]{2,1,0:T(8,128)}), f32[4,64,128]{2,1,0:T(8,128)S(1)}, u32[]{:S(2)}, u32[]{:S(2)}) async-start(f32[4,64,128]{2,1,0:T(8,128)} %get-tuple-element.21), calls=%async_computation.3 | async-start | bytes 262144 | tf_op jit(solution)/shard_map/all_to_all | solution.py:307
  105.2 18.5 %all-to-all-start.4 = ((f32[32,1,128]{2,1,0:T(1,128)}), f32[32,1,128]{2,1,0:T(1,128)S(1)}, u32[]{:S(2)}, u32[]{:S(2)}) async-start(f32[32,1,128]{2,1,0:T(1,128)} %bitcast.4), calls=%async_computation.4 | async-start | bytes 32768 | tf_op jit(solution)/shard_map/all_to_all | solution.py:307

commit v6 on v5

--- a/solution.py
+++ b/solution.py
@@ -210,33 +210,44 @@
         send[i, 64:] = gram
 
 
-def sum_of(chunks, n, total):
-    high, low = total_of([(chunks[i, 64:96], chunks[i, 96:128]) for i in range(n)])
+def value_sum(chunks, n):
     value = chunks[0, :64]
     for i in range(1, n):
         value = value + chunks[i, :64]
-    total[:64] = value
-    total[64:96] = high
-    total[96:128] = low
+    return value
 
 
 def near_sum(chunks, total):
-    sum_of(chunks, 4, total)
+    high, low = total_of([(chunks[i, 64:96], chunks[i, 96:128]) for i in range(4)])
+    high, low = unfold(high), unfold(low)
+    row, lane = places((RANK, RANK))
+    diagonal = jnp.sum(jnp.where(row == lane, low, 0.0), axis=0, keepdims=True)
+    diagonal = jnp.concatenate([diagonal, jnp.zeros((1, 64), F32)], axis=1)
+    total[:64] = value_sum(chunks, 4)
+    total[64:96] = fold(jnp.where(row <= lane, high, low.T))
+    total[96:] = jnp.broadcast_to(diagonal, (8, 128))
 
 
 def far_sum(chunks, copies, gram):
-    high, low = total_of([(chunks[i, 64:96], chunks[i, 96:128]) for i in range(8)])
-    gram[:32] = high
-    gram[32:] = low
-    value = chunks[0, :64]
-    for i in range(1, 8):
-        value = value + chunks[i, :64]
+    value = value_sum(chunks, 8)
     for i in range(4):
         copies[i] = value
+    high, error = total_of([chunks[i, 64:96] for i in range(8)])
+    gram[:32] = high
+    gram[32:64] = error
+    diagonal = chunks[0, 96:]
+    for i in range(1, 8):
+        diagonal = diagonal + chunks[i, 96:]
+    gram[64:] = diagonal
 
 
 def factors(gram, upper_one, inverse_one, inverse_two):
-    high, low = unfold(gram[:32]), unfold(gram[32:])
+    packed, error = unfold(gram[:32]), unfold(gram[32:64])
+    row, lane = places((RANK, RANK))
+    flipped = packed.T
+    high = jnp.where(row <= lane, packed, flipped)
+    low = error + jnp.where(row == lane, gram[64:65, :64], flipped)
+    low = jnp.where(row <= lane, low, low.T)
     upper, inverse = factor(high)
     upper_one[...] = upper
     inverse_one[...] = inverse
@@ -325,11 +336,10 @@
     )
     (copies,) = call(left_tile, [tiled], exchange(part, COL))
     tiles = exchange(copies, COL)
-    chunk = (128, 128)
-    (send,) = call(right_part, [((4,) + chunk, F32)], tiles, blended)
-    (near,) = call(near_sum, [(chunk, F32)], exchange(send, NEAR))
+    (send,) = call(right_part, [((4, 128, 128), F32)], tiles, blended)
+    (near,) = call(near_sum, [((104, 128), F32)], exchange(send, NEAR))
     quarters, gram = call(
-        far_sum, [((4, 64, 128), F32), ((64, 128), F32)], lax.all_gather(near, FAR)
+        far_sum, [((4, 64, 128), F32), ((72, 128), F32)], lax.all_gather(near, FAR)
     )
     total = exchange(quarters, NEAR).reshape(32, 8, 128)
     upper_one, inverse_one, inverse_two = call(factors, [(square, F32)] * 3, gram)

time: 125 us -> 123 us (0.984)
  blocking collectives: 90.7 us -> 87.8 us
    all_gather x1, blocking collectives: 45.1 us -> 42.2 us  [on_device(): lax.all_gather(near, FAR)]
where the time goes in v6:
time: 123 us; the launch traced here: 122 us
  blocking collectives  87.8 us (71%)
  starting transfers between devices  15 us (12%)
  Pallas kernels  13.3 us (11%)
  waiting for transfers between devices  4.79 us (4%)
    all_to_all x3, blocking collectives, exchange(): return lax.all_to_all(chunks, axes, 0, 0, tiled=True)  45.5 us
    all_gather x1, blocking collectives, on_device(): lax.all_gather(near, FAR)  42.2 us
    all_to_all x2, starting transfers between devices, exchange(): return lax.all_to_all(chunks, axes, 0, 0, tiled=True)  15 us
    pallas_call x9, Pallas kernels, call(): pl.pallas_call(kernel, out_shape=[jax.ShapeDtypeStruct(s, d) if i in far_...  13.3 us
    all_to_all x2, waiting for transfers between devices, exchange(): return lax.all_to_all(chunks, axes, 0, 0, tiled=True)  4.79 us
  transfers between devices with their start and end apart: 2, of which 2 were waited for; matrix products, arithmetic and copies ran while one was open for 1% of the time, Pallas kernels for 5%

profile of v6, /device:TPU:1, one launch (start us, length us, event | category | flops | bytes accessed | tf_op | source)
XLA Modules:
  0.0 122.3 jit_solution(15034168755080319900)
XLA Ops:
  0.6 2.5 %left_part.1 = (f32[32,8,128]{2,1,0:T(8,128)S(1)}, f32[512,512]{1,0:T(8,128)S(1)}) custom-call(f32[512,512]{1,0:T(8,128)} %momentum.1, bf16[512,512]{1,0:T(8,128)(2,1)} %gradient.1, f32[64,512]{1,0:T(8,128)} %bitcast.14), custom_call_target="tpu_custom_call" | custom-call | tf_op jit(solution)/shard_map/left_part/pallas_call | solution.py:48
  3.1 24.5 %all_to_all.25.parts = f32[32,8,128]{2,1,0:T(8,128)S(1)} all-to-all(f32[32,8,128]{2,1,0:T(8,128)S(1)} %get-tuple-element.19), channel_id=1, replica_groups=mesh['far'=8,'near'=4,'x'=4,'y'=4,'core'=2] {'x','y','core'}, dimensions={0} | all-to-all | bytes 262144 | tf_op jit(solution)/shard_map/all_to_all | solution.py:318
  27.7 11.2 %all_to_all.26.tiles = f32[32,8,128]{2,1,0:T(8,128)S(1)} all-to-all(f32[32,8,128]{2,1,0:T(8,128)S(1)} %left_tile.1), channel_id=1, replica_groups=mesh['far'=8,'near'=4,'x'=4,'y'=4,'core'=2] {'x','y','core'}, dimensions={0} | all-to-all | bytes 262144 | tf_op jit(solution)/shard_map/all_to_all | solution.py:318
  39.0 1.2 right_part.1
  40.1 9.8 %all_to_all.27.chunks = f32[4,128,128]{2,1,0:T(8,128)S(1)} all-to-all(f32[4,128,128]{2,1,0:T(8,128)S(1)} %right_part.1), channel_id=1, replica_groups=mesh['far'=8,'near'=4,'x'=4,'y'=4,'core'=2] {'near'}, dimensions={0} | all-to-all | bytes 524288 | tf_op jit(solution)/shard_map/all_to_all | solution.py:318
  49.9 0.2 near_sum.1
  50.1 42.2 %all-gather = f32[832,128]{1,0:T(8,128)S(1)} all-gather(f32[104,128]{1,0:T(8,128)S(1)} %near_sum.1), channel_id=2, replica_groups=mesh['far'=8,'near'=4,'x'=4,'y'=4,'core'=2] {'far'}, dimensions={0}, use_global_device_ids=true | all-gather | bytes 479232 | tf_op jit(solution)/shard_map/all_gather | solution.py:342
  92.4 0.7 far_sum.1
  93.0 3.6 %all-to-all-start.3 = ((f32[4,64,128]{2,1,0:T(8,128)}), f32[4,64,128]{2,1,0:T(8,128)S(1)}, u32[]{:S(2)}, u32[]{:S(2)}) async-start(f32[4,64,128]{2,1,0:T(8,128)} %get-tuple-element.21), calls=%async_computation.3 | async-start | bytes 262144 | tf_op jit(solution)/shard_map/all_to_all | solution.py:318
  96.6 4.5 %factors.1 = (f32[64,64]{1,0:T(8,128)S(1)}, f32[64,64]{1,0:T(8,128)S(1)}, f32[64,64]{1,0:T(8,128)S(1)}) custom-call(f32[72,128]{1,0:T(8,128)S(1)} %get-tuple-element.22.gram), custom_call_target="tpu_custom_call" | custom-call | tf_op jit(solution)/shard_map/factors/pallas_call | solution.py:48
  101.1 0.2 all-to-all-done.3
  101.4 1.3 %right_of.1 = (f32[64,512]{1,0:T(8,128)S(1)}, f32[32,128]{1,0:T(8,128)}) custom-call(f32[32,8,128]{2,1,0:T(8,128)S(1)} %bitcast.12, f32[64,64]{1,0:T(8,128)S(1)} %get-tuple-element.23.inverse_one, f32[64,64]{1,0:T(8,128)S(1)} %get-tuple-element.24.inverse_two), custom_call_target="tpu_custom_call" | custom-call | tf_op jit(solution)/shard_map/right_of/pallas_call | solution.py:48
  102.7 11.4 %all-to-all-start.4 = ((f32[32,1,128]{2,1,0:T(1,128)}), f32[32,1,128]{2,1,0:T(1,128)S(1)}, u32[]{:S(2)}, u32[]{:S(2)}) async-start(f32[32,1,128]{2,1,0:T(1,128)} %bitcast.4), calls=%async_computation.4 | async-start | bytes 32768 | tf_op jit(solution)/shard_map/all_to_all | solution.py:318
  114.2 0.7 copy.10
  114.9 1.7 %momentum_of.1 = (f32[64,512]{1,0:T(8,128)S(1)}, f32[64,512]{1,0:T(8,128)}, f32[512,512]{1,0:T(8,128)}) custom-call(f32[32,8,128]{2,1,0:T(8,128)S(1)} %all_to_all.26.tiles, f32[64,64]{1,0:T(8,128)S(1)} %get-tuple-element.23.inverse_one, f32[64,64]{1,0:T(8,128)S(1)} %get-tuple-element.24.inverse_two, f32[64,512]{1,0:T(8,128)S(1)} %get-tuple-element.26.right, ...), custom_call_target="tpu_custom_call" | custom-call | tf_op jit(solution)/shard_map/momentum_of/pallas_call | solution.py:48
  116.6 4.5 %all-to-all-done.4 = f32[32,1,128]{2,1,0:T(1,128)S(1)} async-done(((f32[32,1,128]{2,1,0:T(1,128)}), f32[32,1,128]{2,1,0:T(1,128)S(1)}, u32[]{:S(2)}, u32[]{:S(2)}) %all-to-all-start.4) | async-done | bytes 16416 | tf_op jit(solution)/shard_map/all_to_all | solution.py:318
  121.1 1.1 update_of.1
  (2 shorter events, 0.0 us)
Async XLA Ops:
  93.0 8.3 %all-to-all-start.3 = ((f32[4,64,128]{2,1,0:T(8,128)}), f32[4,64,128]{2,1,0:T(8,128)S(1)}, u32[]{:S(2)}, u32[]{:S(2)}) async-start(f32[4,64,128]{2,1,0:T(8,128)} %get-tuple-element.21), calls=%async_computation.3 | async-start | bytes 262144 | tf_op jit(solution)/shard_map/all_to_all | solution.py:318
  102.7 18.4 %all-to-all-start.4 = ((f32[32,1,128]{2,1,0:T(1,128)}), f32[32,1,128]{2,1,0:T(1,128)S(1)}, u32[]{:S(2)}, u32[]{:S(2)}) async-start(f32[32,1,128]{2,1,0:T(1,128)} %bitcast.4), calls=%async_computation.4 | async-start | bytes 32768 | tf_op jit(solution)/shard_map/all_to_all | solution.py:318
